TPU v7x, 128 devices: a whole 4x4x4 slice. The times are simulated.
128 devices in a mesh: px: 16 (over x, z), py: 8 (over y, core).
Axes of the slice: x: 4, y: 4, z: 4, core: 2. Of those that a mesh axis runs over, the one named last changes fastest.
Arguments:
- coords: float32 [3, 262144], P(None, ('px', 'py')), may hold values from -6 to 6
- displacement: float32 [3, 262144], P(None, ('px', 'py')), may hold values from -3 to 3
- velocity: float32 [3, 262144], P(None, ('px', 'py')), may hold values from -6 to 6
- inv_mass: float32 [262144], P(('px', 'py')), may hold values from 0.5 to 2
- ext_force: float32 [3, 262144], P(None, ('px', 'py')), may hold values from -6 to 6
- thickness: float32 [262144], P(('px', 'py')), may hold values from 0.5 to 2
- stiffness: float32 [12, 12], replicated, may hold values from -12 to 12
- elem_nodes: int32 [4, 262144], P(None, ('px', 'py')), may hold values from 0 to 4095
- block_class: int32 [2048], P(('px', 'py')), may hold values from 0 to 1
- halo_lists: int32 [4, 65536], P(None, ('px', 'py')), may hold values from 0 to 2047
- contact_nodes: int32 [262144], P(('px', 'py')), may hold values from 0 to 2047
- contact_bucket: int32 [262144, 1], P(('px', 'py')), may hold values from 0 to 127; in each aligned block of 2048 rows (0 to 2047, 2048 to 4095, ...) at most 32 rows name the same one
- tile_pairs: int32 [2, 2048], P(None, ('px', 'py')), may hold values from 0 to 31
Outputs:
- disp_out: float32 [3, 262144], P(None, ('px', 'py'))
- vel_out: float32 [3, 262144], P(None, ('px', 'py'))
Inputs may be any that keep to these rules, and one draw needn't show every extreme that they name: `elem_nodes`: indices into the device's extended list: 2048 own nodes, then four blocks of 512 received nodes. `halo_lists`: row 0 is sent to the neighbour one lower along px, row 1 one higher along px, row 2 one lower along py, row 3 one higher along py; entries are own node indices. `block_class`: class of each block of 128 consecutive elements. `contact_nodes`: own node indices of the device. `contact_bucket`: among the 2048 rows of one device no bucket is named more than 32 times, and in every draw some device names some bucket exactly 32 times. `tile_pairs`: tile numbers within the device's own bucket.
All inputs are finite; a program needn't handle non-finite values.
Results may differ from a plain program's by a relative error of at most 0.0003.
Values sent between devices are 32-bit elements; how exact they have to be, the bound alone decides.
A program may use at most 64 MiB of HBM per device.

v0:
```python
import jax
import jax.numpy as jnp
from jax import lax
from jax.sharding import PartitionSpec as P

TILE = 128
EBLK = 128
STEPS = 2
SUBS = 2


FAR = 10000.0
DT = 0.05
PENALTY = 0.5
REACH = 4.0


def padded_2(cells, sides, width):
    for axis, dim in sides:
        count = lax.axis_size(axis)
        ends = count - 1
        head = lax.slice_in_dim(cells, 0, width, axis=dim)
        tail = lax.slice_in_dim(cells, cells.shape[dim] - width, cells.shape[dim], axis=dim)
        cells = jnp.concatenate(
            [
                lax.ppermute(tail, axis, [(i, (i + 1) % count) for i in range(ends)]),
                cells,
                lax.ppermute(head, axis, [((i + 1) % count, i) for i in range(ends)]),
            ],
            axis=dim,
        )
    return cells


def arrange(blocks):
    return jnp.stack([jnp.stack([blocks[0], blocks[3]]), jnp.stack([blocks[2], blocks[1]])])


def extend_edges(values, lists):
    picked = values[:, lists]
    square = arrange([picked[:, 0], picked[:, 1], picked[:, 2], picked[:, 3]])
    padded = padded_2(square, (("px", 0), ("py", 1)), 1)
    return jnp.concatenate([values, padded[0, 2], padded[3, 1], padded[1, 0], padded[2, 3]], axis=1)


def return_edges(force_ext, lists, owned_count):
    halo_width = lists.shape[1]
    blocks = [
        force_ext[:, owned_count + number * halo_width : owned_count + (number + 1) * halo_width]
        for number in range(4)
    ]
    padded = padded_2(arrange(blocks), (("px", 0), ("py", 1)), 1)
    returned = jnp.stack([padded[0, 2], padded[3, 1], padded[1, 0], padded[2, 3]], axis=1).reshape(
        3, -1
    )
    added = jnp.zeros((3, owned_count), jnp.float32).at[:, lists.reshape(-1)].add(returned)
    return force_ext[:, :owned_count] + added


def element_forces(ext_values, elem_nodes, thickness, stiffness):
    corners = ext_values[:, elem_nodes]
    local = corners.reshape(12, elem_nodes.shape[1])
    return thickness[None, :] * jnp.dot(stiffness, local, precision=lax.Precision.HIGHEST)


def assemble(forces, elem_nodes, extended):
    return (
        jnp.zeros((3, extended), jnp.float32)
        .at[:, elem_nodes.reshape(-1)]
        .add(forces.reshape(3, -1))
    )


def contact_slots(bucket, devices, capacity):
    onehot = (bucket[:, None] == jnp.arange(devices, dtype=jnp.int32)[None, :]).astype(jnp.int32)
    before = jnp.cumsum(onehot, axis=0) - onehot
    ranks = jnp.sum(before * onehot, axis=1)
    return bucket * capacity + ranks


def tile_forces(arrived, tile_pairs):
    tiles = arrived.reshape(3, -1, TILE)
    tile_count = tiles.shape[1]
    pair_count = tile_pairs.shape[1]
    group = min(pair_count, 64)
    grouped = tile_pairs.reshape(2, pair_count // group, group).transpose(1, 0, 2)
    numbers = jnp.arange(tile_count, dtype=jnp.int32)

    def one_group(total, pair_group):
        firsts = pair_group[0]
        pos_a = tiles[:, firsts]
        pos_b = tiles[:, pair_group[1]]
        gap = pos_a[:, :, :, None] - pos_b[:, :, None, :]
        dist = jnp.sum(gap * gap, axis=0)
        weight = PENALTY * jnp.exp(-dist / REACH)
        push = jnp.sum(weight[None] * gap, axis=3)
        onehot = (numbers[:, None] == firsts[None, :]).astype(jnp.float32)
        flat = jnp.transpose(push, (1, 0, 2)).reshape(group, 3 * TILE)
        return (total + jnp.dot(onehot, flat, precision=lax.Precision.HIGHEST), None)

    start = jnp.zeros((tile_count, 3 * TILE), jnp.float32)
    total, unused = lax.scan(one_group, start, grouped)
    return jnp.transpose(total.reshape(tile_count, 3, TILE), (1, 0, 2)).reshape(3, -1)


def contact_forces(positions, contact_nodes, slot_ids, tile_pairs, devices, capacity):
    width = devices * capacity
    outgoing = (
        jnp.full((3, width), FAR, jnp.float32).at[:, slot_ids].set(positions[:, contact_nodes])
    )
    arrived = lax.all_to_all(
        outgoing.reshape(3, devices, capacity),
        ("px", "py"),
        split_axis=1,
        concat_axis=1,
        tiled=True,
    ).reshape(3, width)
    pushes = tile_forces(arrived, tile_pairs)
    returned = lax.all_to_all(
        pushes.reshape(3, devices, capacity), ("px", "py"), split_axis=1, concat_axis=1, tiled=True
    ).reshape(3, width)
    return (
        jnp.zeros((3, positions.shape[1]), jnp.float32)
        .at[:, contact_nodes]
        .add(returned[:, slot_ids])
    )


def body(
    coords,
    displacement,
    velocity,
    inv_mass,
    ext_force,
    thickness,
    stiffness,
    elem_nodes,
    block_class,
    halo_lists,
    contact_nodes,
    contact_bucket,
    tile_pairs,
):
    owned_count = coords.shape[1]
    extended = owned_count + 4 * halo_lists.shape[1]
    devices = lax.axis_size("px") * lax.axis_size("py")
    capacity = 2 * contact_nodes.shape[0] // devices
    slot_ids = contact_slots(contact_bucket[:, 0], devices, capacity)
    slow_elems = jnp.repeat(block_class, EBLK) == 1
    for step_no in range(STEPS):
        contact = contact_forces(
            coords + displacement, contact_nodes, slot_ids, tile_pairs, devices, capacity
        )
        held_forces = None
        for sub_no in range(SUBS):
            ext_disp = extend_edges(displacement, halo_lists)
            forces = element_forces(ext_disp, elem_nodes, thickness, stiffness)
            if sub_no == 0:
                held_forces = forces
            else:
                forces = jnp.where(slow_elems[None, :], held_forces, forces)
            internal = return_edges(assemble(forces, elem_nodes, extended), halo_lists, owned_count)
            accel = inv_mass[None, :] * (ext_force - internal + contact)
            velocity = velocity + DT * accel
            displacement = displacement + DT * velocity
    return (displacement, velocity)


def solution(mesh):
    placed = (
        P(None, ("px", "py")),
        P(None, ("px", "py")),
        P(None, ("px", "py")),
        P(("px", "py")),
        P(None, ("px", "py")),
        P(("px", "py")),
        P(),
        P(None, ("px", "py")),
        P(("px", "py")),
        P(None, ("px", "py")),
        P(("px", "py")),
        P(("px", "py"), None),
        P(None, ("px", "py")),
    )
    return jax.shard_map(
        body,
        mesh=mesh,
        in_specs=placed,
        out_specs=(P(None, ("px", "py")), P(None, ("px", "py"))),
        check_vma=False,
    )
```

profile of v0, /device:TPU:2, one launch (start us, length us, event | category | flops | bytes accessed | tf_op | source)
XLA Modules:
  0.0 643.9 jit_solution(17339814742308091553)
XLA Ops:
  19.7 13.1 %scatter_custom_fusion.2 = f32[3,4096]{0,1:T(8,128)S(1)} fusion(s32[2048]{0:T(1024)S(1)} %bitcast.394, f32[3,2048]{0,1:T(8,128)S(1)} %copy.443, s32[2048]{0:T(1024)S(1)} %get-tuple-element.101, f32[]{:T(128)} %constant.24.clone.1), kind=kCustom, calls=%fused_computation.65 | custom fusion | bytes 49156 | tf_op jit(solution)/shard_map/scatter | solution.py:109
  34.4 8.4 %all-to-all-start = ((f32[3,128,32]{2,0,1:T(4,128)}), f32[3,128,32]{2,0,1:T(4,128)S(1)}, u32[]{:S(2)}, u32[]{:S(2)}) async-start(f32[3,128,32]{2,0,1:T(4,128)} %copy.444), calls=%async_computation | async-start | bytes 524288 | tf_op jit(solution)/shard_map/all_to_all | solution.py:111
  52.3 27.7 %gather_fusion.1 = f32[8192,3]{1,0:T(8,128)} fusion(f32[3,4096]{0,1:T(8,128)S(1)} %copy.428, s32[8192]{0:T(1024)S(1)} %broadcast_clamp_fusion), kind=kCustom, calls=%fused_computation.1 | custom fusion | bytes 229376 | tf_op jit(solution)/shard_map/gather | solution.py:61
  86.0 40.9 %scatter_custom_fusion = f32[3,4096]{0,1:T(8,128)S(1)} fusion(s32[8192]{0:T(1024)S(1)} %bitcast.398, f32[3,8192]{0,1:T(8,128)} %copy.430, f32[]{:T(128)} %constant.20.clone.1), kind=kCustom, calls=%fused_computation.38 | custom fusion | flops 24576 | bytes 147460 | tf_op jit(solution)/shard_map/scatter-add | solution.py:70
  143.5 9.0 %all-to-all-start.1 = ((f32[3,128,32]{2,0,1:T(4,128)}), f32[3,128,32]{2,0,1:T(4,128)S(1)}, u32[]{:S(2)}, u32[]{:S(2)}) async-start(f32[3,128,32]{2,0,1:T(4,128)} %copy.452), calls=%async_computation.1 | async-start | bytes 524288 | tf_op jit(solution)/shard_map/all_to_all | solution.py:119
  158.3 11.9 %scatter_fusion = f32[3,2048]{0,1:T(8,128)S(1)} fusion(f32[3,2048]{0,1:T(8,128)S(1)} %slice-done, s32[2048]{0:T(1024)S(1)} %bitcast.364, f32[2048,3]{1,0:T(8,128)S(1)} %bitcast.353), kind=kCustom, calls=%fused_computation.17 | custom fusion | flops 6144 | bytes 81920 | tf_op jit(solution)/shard_map/scatter-add | solution.py:56
  171.9 17.8 %scatter_custom_fusion.3 = f32[3,2048]{0,1:T(8,128)S(1)} fusion(s32[2048]{0:T(1024)} %get-tuple-element.102, f32[3,4096]{0,1:T(8,128)S(1)} %bitcast.351, s32[2048]{0:T(1024)} %broadcast_clamp_fusion.1, f32[]{:T(128)} %constant.20.clone.1), kind=kCustom, calls=%fused_computation.63 | custom fusion | flops 6144 | bytes 25088 | tf_op jit(solution)/shard_map/scatter-add | solution.py:125
  219.3 27.7 %gather_fusion.5 = f32[8192,3]{1,0:T(8,128)} fusion(f32[3,4096]{0,1:T(8,128)S(1)} %copy.465, s32[8192]{0:T(1024)S(1)} %copy-done.4), kind=kCustom, calls=%fused_computation.7 | custom fusion | bytes 229376 | tf_op jit(solution)/shard_map/gather | solution.py:61
  253.0 40.8 %scatter_custom_fusion.4 = f32[3,4096]{0,1:T(8,128)S(1)} fusion(s32[8192]{0:T(1024)} %bitcast.399, f32[3,8192]{0,1:T(8,128)} %copy.467, f32[]{:T(128)} %constant.20.clone.1), kind=kCustom, calls=%fused_computation.36 | custom fusion | flops 24576 | bytes 4243968 | tf_op jit(solution)/shard_map/scatter-add | solution.py:70
  296.4 6.0 collective-permute-start.13
  310.4 11.9 %scatter_fusion.1 = f32[3,2048]{0,1:T(8,128)S(1)} fusion(f32[3,2048]{0,1:T(8,128)S(1)} %slice.424, s32[2048]{0:T(1024)S(1)} %bitcast.365, f32[2048,3]{1,0:T(8,128)S(1)} %bitcast.354), kind=kCustom, calls=%fused_computation.21 | custom fusion | flops 6144 | bytes 81920 | tf_op jit(solution)/shard_map/scatter-add | solution.py:56
  329.5 6.0 collective-permute-start.17
  338.0 13.3 %scatter_custom_fusion.8 = f32[3,4096]{0,1:T(8,128)S(1)} fusion(s32[2048]{0:T(1024)} %bitcast.396, f32[3,2048]{0,1:T(8,128)S(1)} %copy.502, s32[2048]{0:T(1024)} %copy-done.31, f32[]{:T(128)} %constant.24.clone.1), kind=kCustom, calls=%fused_computation.61 | custom fusion | bytes 49664 | tf_op jit(solution)/shard_map/scatter | solution.py:109
  352.8 13.1 %all-to-all-start.2 = ((f32[3,128,32]{2,0,1:T(4,128)}), f32[3,128,32]{2,0,1:T(4,128)S(1)}, u32[]{:S(2)}, u32[]{:S(2)}) async-start(f32[3,128,32]{2,0,1:T(4,128)} %copy.503), calls=%async_computation.2 | async-start | bytes 524288 | tf_op jit(solution)/shard_map/all_to_all | solution.py:111
  372.8 27.7 %gather_fusion.7 = f32[8192,3]{1,0:T(8,128)} fusion(f32[3,4096]{0,1:T(8,128)S(1)} %copy.489, s32[8192]{0:T(1024)S(1)} %copy-done.4), kind=kCustom, calls=%fused_computation.9 | custom fusion | bytes 229376 | tf_op jit(solution)/shard_map/gather | solution.py:61
  406.4 40.8 %scatter_custom_fusion.6 = f32[3,4096]{0,1:T(8,128)S(1)} fusion(s32[8192]{0:T(1024)} %bitcast.400, f32[3,8192]{0,1:T(8,128)} %copy.491, f32[]{:T(128)} %constant.20.clone.1), kind=kCustom, calls=%fused_computation.34 | custom fusion | flops 24576 | bytes 4243968 | tf_op jit(solution)/shard_map/scatter-add | solution.py:70
  463.5 9.0 %all-to-all-start.3 = ((f32[3,128,32]{2,0,1:T(4,128)}), f32[3,128,32]{2,0,1:T(4,128)S(1)}, u32[]{:S(2)}, u32[]{:S(2)}) async-start(f32[3,128,32]{2,0,1:T(4,128)} %copy.511), calls=%async_computation.3 | async-start | bytes 524288 | tf_op jit(solution)/shard_map/all_to_all | solution.py:119
  478.2 12.1 %scatter_fusion.2 = f32[3,2048]{0,1:T(8,128)S(1)} fusion(f32[3,2048]{0,1:T(8,128)S(1)} %slice-done.1, s32[2048]{0:T(1024)S(1)} %bitcast.366, f32[2048,3]{1,0:T(8,128)S(1)} %bitcast.355), kind=kCustom, calls=%fused_computation.23 | custom fusion | flops 6144 | bytes 81920 | tf_op jit(solution)/shard_map/scatter-add | solution.py:56
  492.1 17.8 %scatter_custom_fusion.9 = f32[3,2048]{0,1:T(8,128)S(1)} fusion(s32[2048]{0:T(1024)} %get-tuple-element.102, f32[3,4096]{0,1:T(8,128)S(1)} %bitcast.350, s32[2048]{0:T(1024)} %broadcast_clamp_fusion.1, f32[]{:T(128)} %constant.20.clone.1), kind=kCustom, calls=%fused_computation.59 | custom fusion | flops 6144 | bytes 25088 | tf_op jit(solution)/shard_map/scatter-add | solution.py:125
  524.7 5.7 collective-permute-done.24
  539.5 27.7 %gather_fusion.11 = f32[8192,3]{1,0:T(8,128)} fusion(f32[3,4096]{0,1:T(8,128)S(1)} %copy.524, s32[8192]{0:T(1024)S(1)} %copy-done.5), kind=kCustom, calls=%fused_computation.15 | custom fusion | bytes 229376 | tf_op jit(solution)/shard_map/gather | solution.py:61
  573.2 40.8 %scatter_custom_fusion.10 = f32[3,4096]{0,1:T(8,128)S(1)} fusion(s32[8192]{0:T(1024)} %bitcast.401, f32[3,8192]{0,1:T(8,128)} %copy.526, f32[]{:T(128)} %constant.20.clone.1), kind=kCustom, calls=%fused_computation.32 | custom fusion | flops 24576 | bytes 4243968 | tf_op jit(solution)/shard_map/scatter-add | solution.py:70
  616.5 6.0 collective-permute-start.29
  630.6 11.9 %scatter_fusion.3 = f32[3,2048]{0,1:T(8,128)S(1)} fusion(f32[3,2048]{0,1:T(8,128)S(1)} %slice.466, s32[2048]{0:T(1024)S(1)} %bitcast.367, f32[2048,3]{1,0:T(8,128)S(1)} %bitcast.352), kind=kCustom, calls=%fused_computation.27 | custom fusion | flops 6144 | bytes 81920 | tf_op jit(solution)/shard_map/scatter-add | solution.py:56
  (393 shorter events, 193.0 us)
Async XLA Ops:
  9.7 35.7 %collective-permute-start = (f32[1,2,3,512]{3,1,2,0:T(2,128)S(1)}, f32[1,2,3,512]{3,1,2,0:T(2,128)S(1)}, u32[]{:S(2)}, u32[]{:S(2)}) collective-permute-start(f32[1,2,3,512]{3,1,2,0:T(2,128)S(1)} %maximum_bitcast_fusion), channel_id=1, source_target_pairs={{0,8},{8,16},{16,24},{24,32},{32,40},{40,48},{48,56},{56,64},{64,7... | collective-permute-start | bytes 36872 | tf_op jit(solution)/shard_map/ppermute | solution.py:26
  13.6 31.9 %collective-permute-start.1 = (f32[1,2,3,512]{3,1,2,0:T(2,128)S(1)}, f32[1,2,3,512]{3,1,2,0:T(2,128)S(1)}, u32[]{:S(2)}, u32[]{:S(2)}) collective-permute-start(f32[1,2,3,512]{3,1,2,0:T(2,128)S(1)} %maximum_bitcast_fusion.1), channel_id=1, source_target_pairs={{8,0},{16,8},{24,16},{32,24},{40,32},{48,40},{56,48},{64,56},{72,6... | collective-permute-start | bytes 36872 | tf_op jit(solution)/shard_map/ppermute | solution.py:28
  34.4 103.0 %all-to-all-start = ((f32[3,128,32]{2,0,1:T(4,128)}), f32[3,128,32]{2,0,1:T(4,128)S(1)}, u32[]{:S(2)}, u32[]{:S(2)}) async-start(f32[3,128,32]{2,0,1:T(4,128)} %copy.444), calls=%async_computation | async-start | bytes 524288 | tf_op jit(solution)/shard_map/all_to_all | solution.py:111
  128.7 23.8 %collective-permute-start.4 = (f32[1,2,3,512]{3,1,2,0:T(2,128)S(1)}, f32[1,2,3,512]{3,1,2,0:T(2,128)S(1)}, u32[]{:S(2)}, u32[]{:S(2)}) collective-permute-start(f32[1,2,3,512]{3,1,2,0:T(2,128)S(1)} %maximum_bitcast_fusion.2), channel_id=1, source_target_pairs={{0,8},{8,16},{16,24},{24,32},{32,40},{40,48},{48,56},{56,64},{64,7... | collective-permute-start | bytes 36872 | tf_op jit(solution)/shard_map/ppermute | solution.py:26
  132.6 20.0 %collective-permute-start.5 = (f32[1,2,3,512]{3,1,2,0:T(2,128)S(1)}, f32[1,2,3,512]{3,1,2,0:T(2,128)S(1)}, u32[]{:S(2)}, u32[]{:S(2)}) collective-permute-start(f32[1,2,3,512]{3,1,2,0:T(2,128)S(1)} %maximum_bitcast_fusion.3), channel_id=1, source_target_pairs={{8,0},{16,8},{24,16},{32,24},{40,32},{48,40},{56,48},{64,56},{72,6... | collective-permute-start | bytes 36872 | tf_op jit(solution)/shard_map/ppermute | solution.py:28
  143.5 27.6 %all-to-all-start.1 = ((f32[3,128,32]{2,0,1:T(4,128)}), f32[3,128,32]{2,0,1:T(4,128)S(1)}, u32[]{:S(2)}, u32[]{:S(2)}) async-start(f32[3,128,32]{2,0,1:T(4,128)} %copy.452), calls=%async_computation.1 | async-start | bytes 524288 | tf_op jit(solution)/shard_map/all_to_all | solution.py:119
  197.2 7.3 %collective-permute-start.9 = (f32[1,2,3,512]{3,2,1,0:T(4,128)S(1)}, f32[1,2,3,512]{3,2,1,0:T(4,128)S(1)}, u32[]{:S(2)}, u32[]{:S(2)}) collective-permute-start(f32[1,2,3,512]{3,2,1,0:T(4,128)S(1)} %bitcast.385), channel_id=1, source_target_pairs={{8,0},{16,8},{24,16},{32,24},{40,32},{48,40},{56,48},{64,56},{72,6... | collective-permute-start | bytes 36872 | tf_op jit(solution)/shard_map/ppermute | solution.py:28
  202.5 7.7 %collective-permute-start.8 = (f32[1,2,3,512]{3,2,1,0:T(4,128)S(1)}, f32[1,2,3,512]{3,2,1,0:T(4,128)S(1)}, u32[]{:S(2)}, u32[]{:S(2)}) collective-permute-start(f32[1,2,3,512]{3,2,1,0:T(4,128)S(1)} %bitcast.389), channel_id=1, source_target_pairs={{0,8},{8,16},{16,24},{24,32},{32,40},{40,48},{48,56},{56,64},{64,7... | collective-permute-start | bytes 36872 | tf_op jit(solution)/shard_map/ppermute | solution.py:26
  212.4 6.3 collective-permute-start.11
  294.2 8.4 %collective-permute-start.12 = (f32[1,2,3,512]{3,1,2,0:T(2,128)S(1)}, f32[1,2,3,512]{3,1,2,0:T(2,128)S(1)}, u32[]{:S(2)}, u32[]{:S(2)}) collective-permute-start(f32[1,2,3,512]{3,1,2,0:T(2,128)S(1)} %maximum_bitcast_fusion.4), channel_id=1, source_target_pairs={{0,8},{8,16},{16,24},{24,32},{32,40},{40,48},{48,56},{56,64},{64,7... | collective-permute-start | bytes 36872 | tf_op jit(solution)/shard_map/ppermute | solution.py:26
  296.4 7.4 %collective-permute-start.13 = (f32[1,2,3,512]{3,1,2,0:T(2,128)S(1)}, f32[1,2,3,512]{3,1,2,0:T(2,128)S(1)}, u32[]{:S(2)}, u32[]{:S(2)}) collective-permute-start(f32[1,2,3,512]{3,1,2,0:T(2,128)S(1)} %maximum_bitcast_fusion.5), channel_id=1, source_target_pairs={{8,0},{16,8},{24,16},{32,24},{40,32},{48,40},{56,48},{64,56},{72,6... | collective-permute-start | bytes 36872 | tf_op jit(solution)/shard_map/ppermute | solution.py:28
  303.9 5.3 collective-permute-start.15
  329.5 36.3 %collective-permute-start.17 = (f32[1,2,3,512]{3,2,1,0:T(4,128)S(1)}, f32[1,2,3,512]{3,2,1,0:T(4,128)S(1)}, u32[]{:S(2)}, u32[]{:S(2)}) collective-permute-start(f32[1,2,3,512]{3,2,1,0:T(4,128)S(1)} %bitcast.381), channel_id=1, source_target_pairs={{8,0},{16,8},{24,16},{32,24},{40,32},{48,40},{56,48},{64,56},{72,6... | collective-permute-start | bytes 36872 | tf_op jit(solution)/shard_map/ppermute | solution.py:28
  335.6 30.3 %collective-permute-start.16 = (f32[1,2,3,512]{3,2,1,0:T(4,128)S(1)}, f32[1,2,3,512]{3,2,1,0:T(4,128)S(1)}, u32[]{:S(2)}, u32[]{:S(2)}) collective-permute-start(f32[1,2,3,512]{3,2,1,0:T(4,128)S(1)} %bitcast.383), channel_id=1, source_target_pairs={{0,8},{8,16},{16,24},{24,32},{32,40},{40,48},{48,56},{56,64},{64,7... | collective-permute-start | bytes 36872 | tf_op jit(solution)/shard_map/ppermute | solution.py:26
  352.8 104.6 %all-to-all-start.2 = ((f32[3,128,32]{2,0,1:T(4,128)}), f32[3,128,32]{2,0,1:T(4,128)S(1)}, u32[]{:S(2)}, u32[]{:S(2)}) async-start(f32[3,128,32]{2,0,1:T(4,128)} %copy.503), calls=%async_computation.2 | async-start | bytes 524288 | tf_op jit(solution)/shard_map/all_to_all | solution.py:111
  449.1 23.4 %collective-permute-start.20 = (f32[1,2,3,512]{3,1,2,0:T(2,128)S(1)}, f32[1,2,3,512]{3,1,2,0:T(2,128)S(1)}, u32[]{:S(2)}, u32[]{:S(2)}) collective-permute-start(f32[1,2,3,512]{3,1,2,0:T(2,128)S(1)} %maximum_bitcast_fusion.6), channel_id=1, source_target_pairs={{0,8},{8,16},{16,24},{24,32},{32,40},{40,48},{48,56},{56,64},{64,7... | collective-permute-start | bytes 36872 | tf_op jit(solution)/shard_map/ppermute | solution.py:26
  453.0 19.5 %collective-permute-start.21 = (f32[1,2,3,512]{3,1,2,0:T(2,128)S(1)}, f32[1,2,3,512]{3,1,2,0:T(2,128)S(1)}, u32[]{:S(2)}, u32[]{:S(2)}) collective-permute-start(f32[1,2,3,512]{3,1,2,0:T(2,128)S(1)} %maximum_bitcast_fusion.7), channel_id=1, source_target_pairs={{8,0},{16,8},{24,16},{32,24},{40,32},{48,40},{56,48},{64,56},{72,6... | collective-permute-start | bytes 36872 | tf_op jit(solution)/shard_map/ppermute | solution.py:28
  463.5 27.8 %all-to-all-start.3 = ((f32[3,128,32]{2,0,1:T(4,128)}), f32[3,128,32]{2,0,1:T(4,128)S(1)}, u32[]{:S(2)}, u32[]{:S(2)}) async-start(f32[3,128,32]{2,0,1:T(4,128)} %copy.511), calls=%async_computation.3 | async-start | bytes 524288 | tf_op jit(solution)/shard_map/all_to_all | solution.py:119
  517.4 7.3 %collective-permute-start.25 = (f32[1,2,3,512]{3,2,1,0:T(4,128)S(1)}, f32[1,2,3,512]{3,2,1,0:T(4,128)S(1)}, u32[]{:S(2)}, u32[]{:S(2)}) collective-permute-start(f32[1,2,3,512]{3,2,1,0:T(4,128)S(1)} %bitcast.387), channel_id=1, source_target_pairs={{8,0},{16,8},{24,16},{32,24},{40,32},{48,40},{56,48},{64,56},{72,6... | collective-permute-start | bytes 36872 | tf_op jit(solution)/shard_map/ppermute | solution.py:28
  522.7 7.7 %collective-permute-start.24 = (f32[1,2,3,512]{3,2,1,0:T(4,128)S(1)}, f32[1,2,3,512]{3,2,1,0:T(4,128)S(1)}, u32[]{:S(2)}, u32[]{:S(2)}) collective-permute-start(f32[1,2,3,512]{3,2,1,0:T(4,128)S(1)} %bitcast.391), channel_id=1, source_target_pairs={{0,8},{8,16},{16,24},{24,32},{32,40},{40,48},{48,56},{56,64},{64,7... | collective-permute-start | bytes 36872 | tf_op jit(solution)/shard_map/ppermute | solution.py:26
  532.5 6.3 collective-permute-start.27
  614.4 8.4 %collective-permute-start.28 = (f32[1,2,3,512]{3,1,2,0:T(2,128)S(1)}, f32[1,2,3,512]{3,1,2,0:T(2,128)S(1)}, u32[]{:S(2)}, u32[]{:S(2)}) collective-permute-start(f32[1,2,3,512]{3,1,2,0:T(2,128)S(1)} %maximum_bitcast_fusion.8), channel_id=1, source_target_pairs={{0,8},{8,16},{16,24},{24,32},{32,40},{40,48},{48,56},{56,64},{64,7... | collective-permute-start | bytes 36872 | tf_op jit(solution)/shard_map/ppermute | solution.py:26
  616.5 7.4 %collective-permute-start.29 = (f32[1,2,3,512]{3,1,2,0:T(2,128)S(1)}, f32[1,2,3,512]{3,1,2,0:T(2,128)S(1)}, u32[]{:S(2)}, u32[]{:S(2)}) collective-permute-start(f32[1,2,3,512]{3,1,2,0:T(2,128)S(1)} %maximum_bitcast_fusion.9), channel_id=1, source_target_pairs={{8,0},{16,8},{24,16},{32,24},{40,32},{48,40},{56,48},{64,56},{72,6... | collective-permute-start | bytes 36872 | tf_op jit(solution)/shard_map/ppermute | solution.py:28
  624.1 5.3 collective-permute-start.31
  (51 other events, 802.9 us)
where the time goes:
time: 656 us; the launch traced here: 644 us
  other arithmetic  263 us (40%)
  local copies, waits for them, and re-layouts  209 us (32%)
  starting transfers between devices  135 us (21%)
  waiting for transfers between devices  31.8 us (5%)
    scatter-add x4, other arithmetic, assemble(): return jnp.zeros((3, extended), jnp.float32).at[:, elem_nodes.reshape(-1)...  163 us
    gather x8, local copies, waits for them, and re-layouts, element_forces(): corners = ext_values[:, elem_nodes]  122 us
    ppermute x16, starting transfers between devices, padded_2(): lax.ppermute(head, axis, [((i + 1) % count, i) for i in range(ends)])  52.4 us
    scatter-add x4, other arithmetic, return_edges(): jnp.zeros((3, owned_count), jnp.float32).at[:, lists.reshape(-1)]  47.7 us
    ppermute x16, starting transfers between devices, padded_2(): lax.ppermute(tail, axis, [(i, (i + 1) % count) for i in range(ends)])  42.7 us
    scatter-add x2, other arithmetic, contact_forces(): return jnp.zeros((3, positions.shape[1]), jnp.float32).at[:, contact_node...  35.6 us
    scatter x2, local copies, waits for them, and re-layouts, contact_forces(): jnp.full((3, width), FAR, jnp.float32).at[:, slot_ids]  26.4 us
    gather x8, local copies, waits for them, and re-layouts, extend_edges(): picked = values[:, lists]  23.2 us
  transfers between devices with their start and end apart: 36, of which 12 were waited for; matrix products, arithmetic and copies ran while one was open for 36% of the time, Pallas kernels for 0%

commit v1 on v0

v1 whole, which is shorter than its diff:
```python
import jax
import jax.numpy as jnp
from jax import lax
from jax.experimental import pallas as pl
from jax.experimental.pallas import tpu as pltpu
from jax.sharding import PartitionSpec as P

MESH = pl.DeviceIdType.MESH
LANES = 128
EBLK = 128
STEPS = 2
SUBS = 2
FAR = 10000.0
DT = 0.05
PENALTY = 0.5
REACH = 4.0

N_PX = 16
N_PY = 8
DEVS = N_PX * N_PY
NROW = 16
EROW = 16
HROW = 4
XROW = NROW + 4 * HROW
CROW = 16
SROW = 32
CAP = 32
PAIRS = 16
IDXROW = 4 * EROW + 4 * HROW

F32 = jnp.float32
BF16 = jnp.bfloat16
I32 = jnp.int32


def iota(shape, dim):
    return lax.broadcasted_iota(I32, shape, dim)


def pick(row, index):
    return jnp.take_along_axis(
        jnp.broadcast_to(row, index.shape), index, axis=1, mode="promise_in_bounds"
    )


def gather(table, height, first, count, high, low, start):
    def some(step, found):
        for inner in range(4):
            row = first + step * 4 + inner
            here = high == row
            found = tuple(
                jnp.where(here, pick(table[pl.ds(c * height + row, 1), :], low), found[c])
                for c in range(3)
            )
        return found

    return lax.fori_loop(0, count // 4, some, start)


def halves(value):
    upper = value.astype(BF16).astype(F32)
    return upper, value - upper


def scatter(values, rows, high, first, onehot, tile, height):
    numbers = iota((height, LANES), 0)

    def two_rows(step, total):
        columns = []
        for inner in range(2):
            row = step * 2 + inner
            here = jnp.broadcast_to(high[pl.ds(first + row, 1), :], (height, LANES)) == numbers
            uppers, lowers = [], []
            for c in range(3):
                upper, lower = halves(values[pl.ds(c * rows + row, 1), :])
                uppers.append(jnp.where(here, upper, 0.0))
                lowers.append(jnp.where(here, lower, 0.0))
            columns.append(jnp.concatenate(uppers + lowers, axis=0).astype(BF16))
        left = jnp.concatenate(columns, axis=1)
        return total + jnp.dot(left, onehot[tile + step], preferred_element_type=F32)

    total = lax.fori_loop(0, rows // 2, two_rows, jnp.zeros((6 * height, LANES), F32))
    return total[: 3 * height] + total[3 * height :]


def build_onehots(columns, rows, onehot, tile):
    lanes = iota((LANES, LANES), 1)

    def one(row, carry):
        spread = jnp.take_along_axis(
            columns, jnp.full((LANES, LANES), row, I32), axis=1, mode="promise_in_bounds"
        )
        half = pl.multiple_of(lax.rem(row, 2) * LANES, LANES)
        onehot[tile + row // 2, pl.ds(half, LANES), :] = jnp.where(
            spread == lanes, 1.0, 0.0
        ).astype(BF16)
        return carry

    lax.fori_loop(0, rows, one, 0)


def transposed(index):
    padded = jnp.concatenate(
        [index.astype(F32), jnp.zeros((LANES - index.shape[0], LANES), F32)], axis=0
    )
    return jnp.transpose(padded).astype(I32)


def body(
    coords,
    displacement,
    velocity,
    ext_force,
    elem_nodes,
    halo_lists,
    inv_mass,
    thickness,
    contact_nodes,
    bucket,
    stiffness,
    block_class,
    tile_pairs,
    disp_out,
    vel_out,
    base,
    disp,
    vel,
    fext,
    slow,
    idx_low,
    idx_high,
    table,
    forces,
    held,
    internal,
    contact,
    returned,
    onehot,
    named,
    ranks,
    inverse,
    slot_low,
    slot_high,
    points,
    pushes,
    stage,
    halo_out,
    halo_in,
    back_out,
    back_in,
    slots_out,
    slots_in,
    halo_sent,
    halo_got,
    back_sent,
    back_got,
    slots_sent,
    slots_got,
):
    i = lax.axis_index("px")
    j = lax.axis_index("py")
    me = i * N_PY + j
    neighbours = [
        (i > 0, (jnp.maximum(i - 1, 0), j)),
        (i < N_PX - 1, (jnp.minimum(i + 1, N_PX - 1), j)),
        (j > 0, (i, jnp.maximum(j - 1, 0))),
        (j < N_PY - 1, (i, jnp.minimum(j + 1, N_PY - 1))),
    ]
    facing = [1, 0, 3, 2]

    halo_in[...] = jnp.zeros_like(halo_in)
    back_in[...] = jnp.zeros_like(back_in)

    barrier = pltpu.get_barrier_semaphore()

    def greet(k, carry):
        other = lax.rem(me + k, DEVS)
        pl.semaphore_signal(
            barrier,
            inc=1,
            device_id=(other // N_PY, lax.rem(other, N_PY)),
            device_id_type=MESH,
        )
        return carry

    lax.fori_loop(1, DEVS, greet, 0)

    def to_rows(source, target, count, rows):
        for c in range(count):
            for r in range(rows):
                target[pl.ds(c * rows + r, 1), :] = source[
                    pl.ds(c, 1), pl.ds(r * LANES, LANES)
                ]

    to_rows(coords, base, 3, NROW)
    to_rows(displacement, disp, 3, NROW)
    to_rows(velocity, vel, 3, NROW)
    to_rows(ext_force, fext, 3, NROW)
    for k in range(4):
        for r in range(EROW):
            entry = elem_nodes[pl.ds(k, 1), pl.ds(r * LANES, LANES)]
            idx_low[pl.ds(k * EROW + r, 1), :] = entry & (LANES - 1)
            idx_high[pl.ds(k * EROW + r, 1), :] = entry >> 7
    for k in range(4):
        for r in range(HROW):
            entry = halo_lists[pl.ds(k, 1), pl.ds(r * LANES, LANES)]
            idx_low[pl.ds(4 * EROW + k * HROW + r, 1), :] = entry & (LANES - 1)
            idx_high[pl.ds(4 * EROW + k * HROW + r, 1), :] = entry >> 7
    for r in range(EROW):
        slow[pl.ds(r, 1), :] = jnp.full((1, LANES), block_class[r], I32)

    devs = iota((LANES, LANES), 0)
    lanes = iota((LANES, LANES), 1)
    earlier = jnp.concatenate(
        [jnp.where(devs < lanes, 1.0, 0.0), jnp.ones((LANES, LANES), F32)], axis=1
    ).astype(BF16)

    def rank_row(row, before):
        here = jnp.broadcast_to(bucket[pl.ds(row, 1), :], (LANES, LANES)) == devs
        spread = jnp.where(here, 1.0, 0.0).astype(BF16)
        named[row] = spread
        counts = jnp.dot(spread, earlier, preferred_element_type=F32)
        rank = jnp.sum(
            jnp.where(here, counts[:, :LANES] + before, 0.0), axis=0, keepdims=True
        )
        ranks[pl.ds(row, 1), :] = rank.astype(I32)
        return before + counts[:, LANES:]

    lax.fori_loop(0, CROW, rank_row, jnp.zeros((LANES, LANES), F32))

    joined = transposed(ranks[...] + CAP * contact_nodes[...])
    slot_lane = lanes & (CAP - 1)

    def invert_row(row, total):
        spread = jnp.take_along_axis(
            joined, jnp.full((LANES, LANES), row, I32), axis=1, mode="promise_in_bounds"
        )
        here = (spread & (CAP - 1)) == slot_lane
        low = ((spread >> 5) & (LANES - 1)).astype(F32)
        high = ((spread >> 12) + 1).astype(F32)
        right = jnp.concatenate(
            [jnp.where(here, low, 0.0), jnp.where(here, high, 0.0)], axis=1
        ).astype(BF16)
        return total + jnp.dot(named[row], right, preferred_element_type=F32)

    nodes = lax.fori_loop(0, CROW, invert_row, jnp.zeros((LANES, 2 * LANES), F32))
    inverse[pl.ds(0, DEVS), :] = nodes[:, :LANES]
    inverse[pl.ds(DEVS, DEVS), :] = nodes[:, LANES:]
    block = iota((SROW, LANES), 1) >> 5
    low = jnp.zeros((SROW, LANES), F32)
    high = jnp.zeros((SROW, LANES), F32)
    for q in range(4):
        low = jnp.where(block == q, inverse[pl.ds(q, SROW, stride=4), :], low)
        high = jnp.where(block == q, inverse[pl.ds(DEVS + q, SROW, stride=4), :], high)
    slot_low[...] = low.astype(I32)
    slot_high[...] = high.astype(I32) - 1

    def exchange_start(number, source, target, sent, got):
        for n, (exists, device) in enumerate(neighbours):

            @pl.when(exists)
            def _():
                pltpu.make_async_remote_copy(
                    src_ref=source.at[number, n],
                    dst_ref=target.at[number, facing[n]],
                    send_sem=sent.at[number, n],
                    recv_sem=got.at[number, facing[n]],
                    device_id=device,
                    device_id_type=MESH,
                ).start()

    def exchange_wait(number, buffer, sem):
        for n, (exists, _unused) in enumerate(neighbours):

            @pl.when(exists)
            def _():
                pltpu.make_async_copy(
                    buffer.at[number, n], buffer.at[number, n], sem.at[number, n]
                ).wait()

    def slots_start(number):
        def send(k, carry):
            other = lax.rem(me + k, DEVS)
            pltpu.make_async_remote_copy(
                src_ref=slots_out.at[number, other],
                dst_ref=slots_in.at[number, me],
                send_sem=slots_sent.at[number],
                recv_sem=slots_got.at[number],
                device_id=(other // N_PY, lax.rem(other, N_PY)),
                device_id_type=MESH,
            ).start()
            return carry

        lax.fori_loop(1, DEVS, send, 0)
        slots_in[number, me] = slots_out[number, me]

    def slots_wait(number, buffer, sem):
        part = buffer.at[number, pl.ds(0, DEVS - 1)]
        pltpu.make_async_copy(part, part, sem.at[number]).wait()

    def to_messages(parts, number):
        for q in range(4):
            mixed = jnp.zeros((SROW, LANES), F32)
            for c in range(3):
                shift = (CAP * (c - q)) % LANES
                turned = pltpu.roll(parts[c], shift, 1) if shift else parts[c]
                mixed = jnp.where(block == c, turned, mixed)
            stage[pl.ds(q * SROW, SROW), :] = mixed
        for a in range(SROW):
            for q in range(4):
                slots_out[number, 4 * a + q] = stage[pl.ds(q * SROW + a, 1), :]

    def from_messages(number):
        for a in range(SROW):
            for q in range(4):
                stage[pl.ds(q * SROW + a, 1), :] = slots_in[number, 4 * a + q]
        parts = []
        for c in range(3):
            mixed = jnp.zeros((SROW, LANES), F32)
            for q in range(4):
                shift = (CAP * (q - c)) % LANES
                rows = stage[pl.ds(q * SROW, SROW), :]
                turned = pltpu.roll(rows, shift, 1) if shift else rows
                mixed = jnp.where(block == q, turned, mixed)
            parts.append(mixed)
        return parts

    def send_points(number):
        table[pl.ds(0, 3 * NROW), :] = base[...] + disp[...]
        far = jnp.full((SROW, LANES), FAR, F32)
        found = gather(table, NROW, 0, NROW, slot_high[...], slot_low[...], (far, far, far))
        to_messages(found, number)

    def push_tiles(number):
        for c, part in enumerate(from_messages(number)):
            points[pl.ds(c * SROW, SROW), :] = part
        numbers = iota((SROW, LANES), 0)

        def one_pair(p, totals):
            first = tile_pairs[0, p]
            second = tile_pairs[1, p]
            mine = [
                jnp.broadcast_to(points[pl.ds(c * SROW + first, 1), :], (8, LANES))
                for c in range(3)
            ]
            others = [
                jnp.broadcast_to(points[pl.ds(c * SROW + second, 1), :], (8, LANES))
                for c in range(3)
            ]
            sums = [jnp.zeros((8, LANES), F32) for c in range(3)]
            for turn in range(LANES // 8):
                gap = [
                    mine[c] - pltpu.roll(others[c], turn * 8, 1, stride=1, stride_axis=0)
                    for c in range(3)
                ]
                dist = gap[0] * gap[0] + gap[1] * gap[1] + gap[2] * gap[2]
                weight = PENALTY * jnp.exp(dist * (-1.0 / REACH))
                sums = [sums[c] + weight * gap[c] for c in range(3)]
            return tuple(
                totals[c]
                + jnp.where(numbers == first, jnp.sum(sums[c], axis=0, keepdims=True), 0.0)
                for c in range(3)
            )

        zero = jnp.zeros((SROW, LANES), F32)
        return lax.fori_loop(0, PAIRS, one_pair, (zero, zero, zero))

    def send_edges(number):
        for c in range(3):
            table[pl.ds(c * XROW, NROW), :] = disp[pl.ds(c * NROW, NROW), :]
        zero = jnp.zeros((4 * HROW, LANES), F32)
        listed = pl.ds(4 * EROW, 4 * HROW)
        found = gather(
            table, XROW, 0, NROW, idx_high[listed, :], idx_low[listed, :], (zero, zero, zero)
        )
        for n in range(4):
            for c in range(3):
                halo_out[number, n, pl.ds(c * HROW, HROW), :] = found[c][
                    n * HROW : (n + 1) * HROW
                ]
        exchange_start(number, halo_out, halo_in, halo_sent, halo_got)

    def element_stage(number, sub_no):
        corners = pl.ds(0, 4 * EROW)
        zero = jnp.zeros((4 * EROW, LANES), F32)
        found = gather(
            table, XROW, 0, NROW, idx_high[corners, :], idx_low[corners, :], (zero, zero, zero)
        )
        exchange_wait(number, halo_in, halo_got)
        for n in range(4):
            for c in range(3):
                table[pl.ds(c * XROW + NROW + n * HROW, HROW), :] = halo_in[
                    number, n, pl.ds(c * HROW, HROW), :
                ]
        found = gather(
            table, XROW, NROW, 4 * HROW, idx_high[corners, :], idx_low[corners, :], found
        )
        local = [
            found[c][k * EROW : (k + 1) * EROW] for c in range(3) for k in range(4)
        ]
        thick = thickness[...]
        for out in range(12):
            total = stiffness[out, 0] * local[0]
            for of in range(1, 12):
                total = total + stiffness[out, of] * local[of]
            total = thick * total
            place = pl.ds(out * EROW, EROW)
            if sub_no == 0:
                held[place, :] = total
            else:
                total = jnp.where(slow[...] == 1, held[place, :], total)
            forces[place, :] = total
        summed = scatter(forces, 4 * EROW, idx_high, 0, onehot, 0, XROW)
        for c in range(3):
            internal[pl.ds(c * NROW, NROW), :] = summed[c * XROW : c * XROW + NROW]
            for n in range(4):
                first = c * XROW + NROW + n * HROW
                back_out[number, n, pl.ds(c * HROW, HROW), :] = summed[first : first + HROW]
        exchange_start(number, back_out, back_in, back_sent, back_got)

    def return_stage(number):
        exchange_wait(number, back_in, back_got)
        for n in range(4):
            for c in range(3):
                returned[pl.ds(c * 4 * HROW + n * HROW, HROW), :] = back_in[
                    number, n, pl.ds(c * HROW, HROW), :
                ]
        internal[...] = internal[...] + scatter(
            returned, 4 * HROW, idx_high, 4 * EROW, onehot, 2 * EROW, NROW
        )

    def update():
        mass = inv_mass[...]
        for c in range(3):
            place = pl.ds(c * NROW, NROW)
            accel = mass * (fext[place, :] - internal[place, :] + contact[place, :])
            speed = vel[place, :] + DT * accel
            vel[place, :] = speed
            disp[place, :] = disp[place, :] + DT * speed

    def major(step, carry):
        there, back = 2 * step, 2 * step + 1
        send_points(there)

        @pl.when(step == 0)
        def _():
            pl.semaphore_wait(barrier, DEVS - 1)

        slots_start(there)
        send_edges(there)

        @pl.when(step == 0)
        def _():
            build_onehots(transposed(idx_low[...]), IDXROW, onehot, 0)
            build_onehots(transposed(slot_low[...]), SROW, onehot, IDXROW // 2)

        element_stage(there, 0)
        slots_wait(there, slots_in, slots_got)
        to_messages(push_tiles(there), back)
        slots_start(back)
        return_stage(there)
        slots_wait(back, slots_in, slots_got)
        for c, part in enumerate(from_messages(back)):
            pushes[pl.ds(c * SROW, SROW), :] = part
        contact[...] = scatter(pushes, SROW, slot_high, 0, onehot, IDXROW // 2, NROW)
        update()
        for sub_no in range(1, SUBS):
            send_edges(back)
            element_stage(back, sub_no)
            return_stage(back)
            update()
        return carry

    lax.fori_loop(0, STEPS, major, 0)

    for c in range(3):
        for r in range(NROW):
            row = pl.ds(c * NROW + r, 1)
            place = pl.ds(r * LANES, LANES)
            disp_out[pl.ds(c, 1), place] = disp[row, :]
            vel_out[pl.ds(c, 1), place] = vel[row, :]

    def drain(number, carry):
        exchange_wait(number, halo_out, halo_sent)
        exchange_wait(number, back_out, back_sent)
        slots_wait(number, slots_out, slots_sent)
        return carry

    lax.fori_loop(0, STEPS * SUBS, drain, 0)


def device_step(
    coords,
    displacement,
    velocity,
    inv_mass,
    ext_force,
    thickness,
    stiffness,
    elem_nodes,
    block_class,
    halo_lists,
    contact_nodes,
    contact_bucket,
    tile_pairs,
):
    times = STEPS * SUBS
    vmem = pl.BlockSpec(memory_space=pltpu.VMEM)
    smem = pl.BlockSpec(memory_space=pltpu.SMEM)
    dma = pltpu.SemaphoreType.DMA
    shape = jax.ShapeDtypeStruct(coords.shape, F32)
    rows = lambda count, kind=F32: pltpu.VMEM((count, LANES), kind)
    edges = pltpu.VMEM((times, 4, 3 * HROW, LANES), F32)
    messages = pltpu.VMEM((times, DEVS, 1, LANES), F32)
    return pl.pallas_call(
        body,
        out_shape=(shape, shape),
        in_specs=[vmem] * 10 + [smem] * 3,
        out_specs=(vmem, vmem),
        scratch_shapes=[
            rows(3 * NROW),
            rows(3 * NROW),
            rows(3 * NROW),
            rows(3 * NROW),
            rows(EROW, I32),
            rows(IDXROW, I32),
            rows(IDXROW, I32),
            rows(3 * XROW),
            rows(12 * EROW),
            rows(12 * EROW),
            rows(3 * NROW),
            rows(3 * NROW),
            rows(12 * HROW),
            pltpu.VMEM(((IDXROW + SROW) // 2, 2 * LANES, LANES), BF16),
            pltpu.VMEM((CROW, DEVS, LANES), BF16),
            rows(CROW, I32),
            rows(2 * DEVS),
            rows(SROW, I32),
            rows(SROW, I32),
            rows(3 * SROW),
            rows(3 * SROW),
            rows(DEVS),
            edges,
            edges,
            edges,
            edges,
            messages,
            messages,
            dma((times, 4)),
            dma((times, 4)),
            dma((times, 4)),
            dma((times, 4)),
            dma((times,)),
            dma((times,)),
        ],
        compiler_params=pltpu.CompilerParams(
            collective_id=0, has_side_effects=True, vmem_limit_bytes=40 * 1024 * 1024
        ),
    )(
        coords,
        displacement,
        velocity,
        ext_force,
        elem_nodes,
        halo_lists,
        inv_mass.reshape(NROW, LANES),
        thickness.reshape(EROW, LANES),
        contact_nodes.reshape(CROW, LANES),
        contact_bucket.reshape(CROW, LANES),
        stiffness,
        block_class,
        tile_pairs,
    )


def solution(mesh):
    split = P(None, ("px", "py"))
    line = P(("px", "py"))
    placed = (
        split,
        split,
        split,
        line,
        split,
        line,
        P(),
        split,
        line,
        split,
        line,
        P(("px", "py"), None),
        split,
    )
    return jax.shard_map(
        device_step,
        mesh=mesh,
        in_specs=placed,
        out_specs=(split, split),
        check_vma=False,
    )
```

time: 656 us -> 117 us (0.18); the launches traced: 644 us -> 117 us
  other arithmetic: 263 us -> 0 us
  local copies, waits for them, and re-layouts: 209 us -> 9.86 us
  starting transfers between devices: 135 us -> 0 us
  Pallas kernels: 0 us -> 106 us
  waiting for transfers between devices: 31.8 us -> 0 us
    scatter-add x10 -> x0, other arithmetic: 247 us -> none  [the longest x4 163 us: assemble(): return jnp.zeros((3, extended), jnp.float32).at[:, elem_nodes.reshape(-1)...]
    gather x24 -> x0, local copies, waits for them, and re-layouts: 148 us -> none  [the longest x8 122 us: element_forces(): corners = ext_values[:, elem_nodes]]
    pallas_call x0 -> x1, Pallas kernels: none -> 106 us  [device_step(): pl.pallas_call(body, out_shape=(shape, shape), in_specs=[vmem] * 10 + [sm...]
    ppermute x32 -> x0, starting transfers between devices: 95.1 us -> none  [the longest x16 52.4 us: padded_2(): lax.ppermute(head, axis, [((i + 1) % count, i) for i in range(ends)])]
    all_to_all x4 -> x0, starting transfers between devices: 39.5 us -> none  [the longest x2 21.5 us: contact_forces(): lax.all_to_all(outgoing.reshape(3, devices, capacity), ('px', 'py'), spli...]
    ppermute x32 -> x0, waiting for transfers between devices: 31.8 us -> none  [the longest x16 17.3 us: padded_2(): lax.ppermute(head, axis, [((i + 1) % count, i) for i in range(ends)])]
    scatter x2 -> x0, local copies, waits for them, and re-layouts: 26.4 us -> none  [contact_forces(): jnp.full((3, width), FAR, jnp.float32).at[:, slot_ids]]
    reshape x18 -> x0, local copies, waits for them, and re-layouts: 15.6 us -> none  [the longest x8 10.9 us: assemble(): forces.reshape(3, -1)]
  transfers between devices with their start and end apart: 36 -> 0, of which waited for: 12 -> 0; matrix products, arithmetic and copies ran while one was open for 36% -> 0% of each run, Pallas kernels for 0% -> 0%
where the time goes in v1:
time: 117 us
  Pallas kernels  106 us (91%)
  local copies, waits for them, and re-layouts  9.86 us (8%)
    pallas_call x1, Pallas kernels, device_step(): pl.pallas_call(body, out_shape=(shape, shape), in_specs=[vmem] * 10 + [sm...  106 us
    unnamed x28, local copies, waits for them, and re-layouts  9.86 us

profile of v1, /device:TPU:2, one launch (start us, length us, event | category | flops | bytes accessed | tf_op | source)
XLA Modules:
  0.0 116.8 jit_solution(8906688830931981284)
XLA Ops:
  0.6 0.0 copy-start.11
  0.6 0.0 copy-start.12
  0.7 0.7 copy-done.11
  1.3 0.0 copy-done.12
  1.3 0.0 copy-start
  1.3 0.8 copy-done
  2.1 0.8 copy-done.1
  2.8 0.0 copy-start.2
  2.8 0.8 copy-done.2
  3.6 0.0 copy-start.3
  3.6 0.8 copy-done.3
  4.4 0.0 copy-start.4
  4.4 0.8 copy-done.4
  5.1 0.0 copy-start.5
  5.1 0.7 copy-done.5
  5.8 0.0 copy-start.6
  5.8 0.7 copy-done.6
  6.5 0.7 copy-done.7
  7.2 0.7 copy-done.8
  7.9 0.7 copy-done.9
  8.6 0.7 copy-done.10
  9.3 106.2 %shard_map.140 = (f32[3,2048]{1,0:T(4,128)S(1)}, f32[3,2048]{1,0:T(4,128)S(1)}) custom-call(f32[3,2048]{1,0:T(4,128)S(1)} %copy-done, f32[3,2048]{1,0:T(4,128)S(1)} %copy-done.1, f32[3,2048]{1,0:T(4,128)S(1)} %copy-done.2, f32[3,2048]{1,0:T(4,128)S(1)} %copy-done.3, s32[4,2048]{1,0:T(4,128)S(1)} %copy-done.4, s32[4,512]{1,0:T(4,128)S(1)} %copy-done.5, ...), custom_call_target="tpu_custom_call" | custom-call | tf_op jit(solution)/shard_map/pallas_call | solution.py:515
  115.5 0.6 copy.17
  116.2 0.6 copy.18
  (5 shorter events, 0.0 us)
Async XLA Ops:
  0.6 0.7 copy-start.11
  0.6 0.7 copy-start.12
  1.3 0.8 copy-start
  2.1 0.8 copy-start.1
  2.8 0.8 copy-start.2
  3.6 0.8 copy-start.3
  4.4 0.8 copy-start.4
  5.1 0.7 copy-start.5
  5.8 0.7 copy-start.6
  6.5 0.7 copy-start.7
  7.2 0.7 copy-start.8
  7.9 0.7 copy-start.9
  8.6 0.7 copy-start.10

commit v2 on v1

--- a/solution.py
+++ b/solution.py
@@ -27,6 +27,7 @@
 CAP = 32
 PAIRS = 16
 IDXROW = 4 * EROW + 4 * HROW
+UNROLL = 4
 
 F32 = jnp.float32
 BF16 = jnp.bfloat16
@@ -37,76 +38,107 @@
     return lax.broadcasted_iota(I32, shape, dim)
 
 
-def pick(row, index):
-    return jnp.take_along_axis(
-        jnp.broadcast_to(row, index.shape), index, axis=1, mode="promise_in_bounds"
-    )
-
-
-def gather(table, height, first, count, high, low, start):
-    def some(step, found):
-        for inner in range(4):
-            row = first + step * 4 + inner
-            here = high == row
-            found = tuple(
-                jnp.where(here, pick(table[pl.ds(c * height + row, 1), :], low), found[c])
-                for c in range(3)
-            )
-        return found
-
-    return lax.fori_loop(0, count // 4, some, start)
-
-
 def halves(value):
     upper = value.astype(BF16).astype(F32)
     return upper, value - upper
 
 
-def scatter(values, rows, high, first, onehot, tile, height):
-    numbers = iota((height, LANES), 0)
-
-    def two_rows(step, total):
-        columns = []
-        for inner in range(2):
-            row = step * 2 + inner
-            here = jnp.broadcast_to(high[pl.ds(first + row, 1), :], (height, LANES)) == numbers
-            uppers, lowers = [], []
-            for c in range(3):
-                upper, lower = halves(values[pl.ds(c * rows + row, 1), :])
-                uppers.append(jnp.where(here, upper, 0.0))
-                lowers.append(jnp.where(here, lower, 0.0))
-            columns.append(jnp.concatenate(uppers + lowers, axis=0).astype(BF16))
-        left = jnp.concatenate(columns, axis=1)
-        return total + jnp.dot(left, onehot[tile + step], preferred_element_type=F32)
-
-    total = lax.fori_loop(0, rows // 2, two_rows, jnp.zeros((6 * height, LANES), F32))
+def gather(tables, place, rows, high, first, onehot, number, found, target, add):
+    numbers = iota((NROW, LANES), 0) + place
+
+    def some(step, carry):
+        for inner in range(UNROLL):
+            tile = step * UNROLL + inner
+            both = jnp.dot(tables, onehot[number + tile], preferred_element_type=F32)
+            for side in range(2):
+                row = tile * 2 + side
+                here = jnp.broadcast_to(high[pl.ds(first + row, 1), :], (NROW, LANES)) == numbers
+                for c in range(3):
+                    part = both[c * NROW : (c + 1) * NROW, side * LANES : (side + 1) * LANES]
+                    total = jnp.sum(jnp.where(here, part, 0.0), axis=0, keepdims=True)
+                    spot = pl.ds(target + c * rows + row, 1)
+                    found[spot, :] = found[spot, :] + total if add else total
+        return carry
+
+    lax.fori_loop(0, rows // (2 * UNROLL), some, 0)
+
+
+def split_table(table):
+    return jnp.concatenate(halves(table), axis=1).astype(BF16)
+
+
+def scatter(values, halved, rows, high, first, onehot, number, height):
+    upper, lower = halves(values[pl.ds(0, 3 * rows), :])
+    halved[pl.ds(0, 3 * rows), :] = upper
+    halved[pl.ds(3 * rows, 3 * rows), :] = lower
+    numbers = iota((16, LANES), 0).astype(F32).astype(BF16)
+
+    def some(step, total):
+        columns, right = [], []
+        for inner in range(2 * UNROLL):
+            row = step * 2 * UNROLL + inner
+            mine = jnp.broadcast_to(high[pl.ds(first + row, 1), :], (16, LANES))
+            mine = mine.astype(F32).astype(BF16)
+            here = [mine == numbers + 16 * k for k in range(height // 16)]
+            parts = []
+            for part in range(6):
+                value = jnp.broadcast_to(
+                    halved[pl.ds(part * rows + row, 1), :], (16, LANES)
+                ).astype(BF16)
+                parts += [jnp.where(mask, value, jnp.zeros_like(value)) for mask in here]
+            columns.append(jnp.concatenate(parts, axis=0))
+        for inner in range(UNROLL):
+            right.append(onehot[number + step * UNROLL + inner, pl.ds(0, LANES), :])
+        return total + lax.dot_general(
+            jnp.concatenate(columns, axis=1),
+            jnp.concatenate(right, axis=1),
+            (((1,), (1,)), ((), ())),
+            preferred_element_type=F32,
+        )
+
+    total = lax.fori_loop(
+        0, rows // (2 * UNROLL), some, jnp.zeros((6 * height, LANES), F32)
+    )
     return total[: 3 * height] + total[3 * height :]
 
 
-def build_onehots(columns, rows, onehot, tile):
-    lanes = iota((LANES, LANES), 1)
-
-    def one(row, carry):
-        spread = jnp.take_along_axis(
-            columns, jnp.full((LANES, LANES), row, I32), axis=1, mode="promise_in_bounds"
-        )
-        half = pl.multiple_of(lax.rem(row, 2) * LANES, LANES)
-        onehot[tile + row // 2, pl.ds(half, LANES), :] = jnp.where(
-            spread == lanes, 1.0, 0.0
-        ).astype(BF16)
+def build_onehots(low, first, rows, onehot, number):
+    numbers = iota((LANES, LANES), 0)
+
+    def some(step, carry):
+        for inner in range(UNROLL):
+            tile = step * UNROLL + inner
+            for side in range(2):
+                mine = low[pl.ds(first + tile * 2 + side, 1), :]
+                here = jnp.broadcast_to(mine, (LANES, LANES)) == numbers
+                ones = jnp.where(here, 1.0, 0.0).astype(BF16)
+                for copy in range(2):
+                    onehot[
+                        number + tile,
+                        pl.ds(copy * LANES, LANES),
+                        pl.ds(side * LANES, LANES),
+                    ] = ones
         return carry
 
-    lax.fori_loop(0, rows, one, 0)
-
-
-def transposed(index):
-    padded = jnp.concatenate(
-        [index.astype(F32), jnp.zeros((LANES - index.shape[0], LANES), F32)], axis=0
-    )
-    return jnp.transpose(padded).astype(I32)
+    lax.fori_loop(0, rows // (2 * UNROLL), some, 0)
 
 
 def body(
+    coords_hbm,
+    displacement_hbm,
+    velocity_hbm,
+    ext_force_hbm,
+    elem_nodes_hbm,
+    halo_lists_hbm,
+    inv_mass_hbm,
+    thickness_hbm,
+    contact_nodes_hbm,
+    bucket_hbm,
+    stiffness_hbm,
+    block_class_hbm,
+    tile_pairs_hbm,
+    disp_out,
+    vel_out,
     coords,
     displacement,
     velocity,
@@ -120,24 +152,23 @@
     stiffness,
     block_class,
     tile_pairs,
-    disp_out,
-    vel_out,
     base,
     disp,
     vel,
     fext,
     slow,
+    spread,
     idx_low,
     idx_high,
-    table,
+    found,
     forces,
     held,
+    halved,
     internal,
     contact,
     returned,
+    ghosts,
     onehot,
-    named,
-    ranks,
     inverse,
     slot_low,
     slot_high,
@@ -150,6 +181,7 @@
     back_in,
     slots_out,
     slots_in,
+    loads,
     halo_sent,
     halo_got,
     back_sent,
@@ -157,6 +189,43 @@
     slots_sent,
     slots_got,
 ):
+    sources = [
+        bucket_hbm,
+        contact_nodes_hbm,
+        coords_hbm,
+        displacement_hbm,
+        halo_lists_hbm,
+        elem_nodes_hbm,
+        velocity_hbm,
+        ext_force_hbm,
+        inv_mass_hbm,
+        thickness_hbm,
+        stiffness_hbm,
+        block_class_hbm,
+        tile_pairs_hbm,
+    ]
+    targets = [
+        bucket,
+        contact_nodes,
+        coords,
+        displacement,
+        halo_lists,
+        elem_nodes,
+        velocity,
+        ext_force,
+        inv_mass,
+        thickness,
+        stiffness,
+        block_class,
+        tile_pairs,
+    ]
+    copies = [
+        pltpu.make_async_copy(source, target, loads.at[n])
+        for n, (source, target) in enumerate(zip(sources, targets))
+    ]
+    for copy in copies:
+        copy.start()
+
     i = lax.axis_index("px")
     j = lax.axis_index("py")
     me = i * N_PY + j
@@ -192,58 +261,45 @@
                     pl.ds(c, 1), pl.ds(r * LANES, LANES)
                 ]
 
-    to_rows(coords, base, 3, NROW)
-    to_rows(displacement, disp, 3, NROW)
-    to_rows(velocity, vel, 3, NROW)
-    to_rows(ext_force, fext, 3, NROW)
-    for k in range(4):
-        for r in range(EROW):
-            entry = elem_nodes[pl.ds(k, 1), pl.ds(r * LANES, LANES)]
-            idx_low[pl.ds(k * EROW + r, 1), :] = entry & (LANES - 1)
-            idx_high[pl.ds(k * EROW + r, 1), :] = entry >> 7
-    for k in range(4):
-        for r in range(HROW):
-            entry = halo_lists[pl.ds(k, 1), pl.ds(r * LANES, LANES)]
-            idx_low[pl.ds(4 * EROW + k * HROW + r, 1), :] = entry & (LANES - 1)
-            idx_high[pl.ds(4 * EROW + k * HROW + r, 1), :] = entry >> 7
-    for r in range(EROW):
-        slow[pl.ds(r, 1), :] = jnp.full((1, LANES), block_class[r], I32)
-
     devs = iota((LANES, LANES), 0)
     lanes = iota((LANES, LANES), 1)
     earlier = jnp.concatenate(
         [jnp.where(devs < lanes, 1.0, 0.0), jnp.ones((LANES, LANES), F32)], axis=1
     ).astype(BF16)
-
-    def rank_row(row, before):
+    copies[0].wait()
+    before = jnp.zeros((LANES, LANES), F32)
+    named, ranks = [], []
+    for row in range(CROW):
         here = jnp.broadcast_to(bucket[pl.ds(row, 1), :], (LANES, LANES)) == devs
-        spread = jnp.where(here, 1.0, 0.0).astype(BF16)
-        named[row] = spread
-        counts = jnp.dot(spread, earlier, preferred_element_type=F32)
-        rank = jnp.sum(
-            jnp.where(here, counts[:, :LANES] + before, 0.0), axis=0, keepdims=True
-        )
-        ranks[pl.ds(row, 1), :] = rank.astype(I32)
-        return before + counts[:, LANES:]
-
-    lax.fori_loop(0, CROW, rank_row, jnp.zeros((LANES, LANES), F32))
-
-    joined = transposed(ranks[...] + CAP * contact_nodes[...])
-    slot_lane = lanes & (CAP - 1)
-
-    def invert_row(row, total):
-        spread = jnp.take_along_axis(
-            joined, jnp.full((LANES, LANES), row, I32), axis=1, mode="promise_in_bounds"
-        )
-        here = (spread & (CAP - 1)) == slot_lane
-        low = ((spread >> 5) & (LANES - 1)).astype(F32)
-        high = ((spread >> 12) + 1).astype(F32)
-        right = jnp.concatenate(
-            [jnp.where(here, low, 0.0), jnp.where(here, high, 0.0)], axis=1
-        ).astype(BF16)
-        return total + jnp.dot(named[row], right, preferred_element_type=F32)
-
-    nodes = lax.fori_loop(0, CROW, invert_row, jnp.zeros((LANES, 2 * LANES), F32))
+        ones = jnp.where(here, 1.0, 0.0).astype(BF16)
+        counts = jnp.dot(ones, earlier, preferred_element_type=F32)
+        ranks.append(
+            jnp.sum(jnp.where(here, counts[:, :LANES] + before, 0.0), axis=0, keepdims=True)
+        )
+        before = before + counts[:, LANES:]
+        named.append(ones)
+
+    copies[1].wait()
+    slot_row = (devs & (CAP - 1)).astype(F32)
+    nodes = jnp.zeros((LANES, 2 * LANES), F32)
+    for row in range(0, CROW, 2):
+        right = []
+        for one in (row, row + 1):
+            here = jnp.broadcast_to(ranks[one], (LANES, LANES)) == slot_row
+            node = contact_nodes[pl.ds(one, 1), :]
+            low = jnp.broadcast_to((node & (LANES - 1)).astype(F32), (LANES, LANES))
+            high = jnp.broadcast_to(((node >> 7) + 1).astype(F32), (LANES, LANES))
+            right.append(
+                jnp.concatenate(
+                    [jnp.where(here, low, 0.0), jnp.where(here, high, 0.0)], axis=0
+                ).astype(BF16)
+            )
+        nodes = nodes + lax.dot_general(
+            jnp.concatenate([named[row], named[row + 1]], axis=1),
+            jnp.concatenate(right, axis=1),
+            (((1,), (1,)), ((), ())),
+            preferred_element_type=F32,
+        )
     inverse[pl.ds(0, DEVS), :] = nodes[:, :LANES]
     inverse[pl.ds(DEVS, DEVS), :] = nodes[:, LANES:]
     block = iota((SROW, LANES), 1) >> 5
@@ -254,6 +310,39 @@
         high = jnp.where(block == q, inverse[pl.ds(DEVS + q, SROW, stride=4), :], high)
     slot_low[...] = low.astype(I32)
     slot_high[...] = high.astype(I32) - 1
+    build_onehots(slot_low, 0, SROW, onehot, IDXROW // 2)
+
+    copies[2].wait()
+    copies[3].wait()
+    to_rows(coords, base, 3, NROW)
+    to_rows(displacement, disp, 3, NROW)
+
+    def prepare_halo():
+        copies[4].wait()
+        for k in range(4):
+            for r in range(HROW):
+                entry = halo_lists[pl.ds(k, 1), pl.ds(r * LANES, LANES)]
+                idx_low[pl.ds(4 * EROW + k * HROW + r, 1), :] = entry & (LANES - 1)
+                idx_high[pl.ds(4 * EROW + k * HROW + r, 1), :] = entry >> 7
+        build_onehots(idx_low, 4 * EROW, 4 * HROW, onehot, 2 * EROW)
+
+    def prepare_rest():
+        for copy in copies[5:]:
+            copy.wait()
+        for k in range(4):
+            for r in range(EROW):
+                entry = elem_nodes[pl.ds(k, 1), pl.ds(r * LANES, LANES)]
+                idx_low[pl.ds(k * EROW + r, 1), :] = entry & (LANES - 1)
+                idx_high[pl.ds(k * EROW + r, 1), :] = entry >> 7
+        build_onehots(idx_low, 0, 4 * EROW, onehot, 0)
+        to_rows(velocity, vel, 3, NROW)
+        to_rows(ext_force, fext, 3, NROW)
+        for r in range(EROW):
+            slow[pl.ds(r, 1), :] = jnp.full((1, LANES), block_class[r], I32)
+        for column in range(12):
+            spread[pl.ds(column * 16, 12), :] = jnp.broadcast_to(
+                stiffness[:, column : column + 1], (12, LANES)
+            )
 
     def exchange_start(number, source, target, sent, got):
         for n, (exists, device) in enumerate(neighbours):
@@ -326,10 +415,23 @@
         return parts
 
     def send_points(number):
-        table[pl.ds(0, 3 * NROW), :] = base[...] + disp[...]
-        far = jnp.full((SROW, LANES), FAR, F32)
-        found = gather(table, NROW, 0, NROW, slot_high[...], slot_low[...], (far, far, far))
-        to_messages(found, number)
+        gather(
+            split_table(base[...] + disp[...]),
+            0,
+            SROW,
+            slot_high,
+            0,
+            onehot,
+            IDXROW // 2,
+            points,
+            0,
+            False,
+        )
+        empty = slot_high[...] < 0
+        to_messages(
+            [jnp.where(empty, FAR, points[pl.ds(c * SROW, SROW), :]) for c in range(3)],
+            number,
+        )
 
     def push_tiles(number):
         for c, part in enumerate(from_messages(number)):
@@ -366,43 +468,47 @@
         return lax.fori_loop(0, PAIRS, one_pair, (zero, zero, zero))
 
     def send_edges(number):
-        for c in range(3):
-            table[pl.ds(c * XROW, NROW), :] = disp[pl.ds(c * NROW, NROW), :]
-        zero = jnp.zeros((4 * HROW, LANES), F32)
-        listed = pl.ds(4 * EROW, 4 * HROW)
-        found = gather(
-            table, XROW, 0, NROW, idx_high[listed, :], idx_low[listed, :], (zero, zero, zero)
+        gather(
+            split_table(disp[...]),
+            0,
+            4 * HROW,
+            idx_high,
+            4 * EROW,
+            onehot,
+            2 * EROW,
+            returned,
+            0,
+            False,
         )
         for n in range(4):
             for c in range(3):
-                halo_out[number, n, pl.ds(c * HROW, HROW), :] = found[c][
-                    n * HROW : (n + 1) * HROW
+                halo_out[number, n, pl.ds(c * HROW, HROW), :] = returned[
+                    pl.ds((c * 4 + n) * HROW, HROW), :
                 ]
         exchange_start(number, halo_out, halo_in, halo_sent, halo_got)
 
+    def own_corners():
+        gather(
+            split_table(disp[...]), 0, 4 * EROW, idx_high, 0, onehot, 0, found, 0, False
+        )
+
     def element_stage(number, sub_no):
-        corners = pl.ds(0, 4 * EROW)
-        zero = jnp.zeros((4 * EROW, LANES), F32)
-        found = gather(
-            table, XROW, 0, NROW, idx_high[corners, :], idx_low[corners, :], (zero, zero, zero)
-        )
         exchange_wait(number, halo_in, halo_got)
         for n in range(4):
             for c in range(3):
-                table[pl.ds(c * XROW + NROW + n * HROW, HROW), :] = halo_in[
+                ghosts[pl.ds((c * 4 + n) * HROW, HROW), :] = halo_in[
                     number, n, pl.ds(c * HROW, HROW), :
                 ]
-        found = gather(
-            table, XROW, NROW, 4 * HROW, idx_high[corners, :], idx_low[corners, :], found
-        )
-        local = [
-            found[c][k * EROW : (k + 1) * EROW] for c in range(3) for k in range(4)
-        ]
+        gather(
+            split_table(ghosts[...]), NROW, 4 * EROW, idx_high, 0, onehot, 0, found, 0, True
+        )
+        local = [found[pl.ds(n * EROW, EROW), :] for n in range(12)]
         thick = thickness[...]
         for out in range(12):
-            total = stiffness[out, 0] * local[0]
-            for of in range(1, 12):
-                total = total + stiffness[out, of] * local[of]
+            total = jnp.zeros((EROW, LANES), F32)
+            for of in range(12):
+                factor = spread[pl.ds(of * 16 + out, 1), :]
+                total = total + jnp.broadcast_to(factor, (EROW, LANES)) * local[of]
             total = thick * total
             place = pl.ds(out * EROW, EROW)
             if sub_no == 0:
@@ -410,7 +516,7 @@
             else:
                 total = jnp.where(slow[...] == 1, held[place, :], total)
             forces[place, :] = total
-        summed = scatter(forces, 4 * EROW, idx_high, 0, onehot, 0, XROW)
+        summed = scatter(forces, halved, 4 * EROW, idx_high, 0, onehot, 0, XROW)
         for c in range(3):
             internal[pl.ds(c * NROW, NROW), :] = summed[c * XROW : c * XROW + NROW]
             for n in range(4):
@@ -426,7 +532,7 @@
                     number, n, pl.ds(c * HROW, HROW), :
                 ]
         internal[...] = internal[...] + scatter(
-            returned, 4 * HROW, idx_high, 4 * EROW, onehot, 2 * EROW, NROW
+            returned, halved, 4 * HROW, idx_high, 4 * EROW, onehot, 2 * EROW, NROW
         )
 
     def update():
@@ -447,13 +553,10 @@
             pl.semaphore_wait(barrier, DEVS - 1)
 
         slots_start(there)
+        pl.when(step == 0)(prepare_halo)
         send_edges(there)
-
-        @pl.when(step == 0)
-        def _():
-            build_onehots(transposed(idx_low[...]), IDXROW, onehot, 0)
-            build_onehots(transposed(slot_low[...]), SROW, onehot, IDXROW // 2)
-
+        pl.when(step == 0)(prepare_rest)
+        own_corners()
         element_stage(there, 0)
         slots_wait(there, slots_in, slots_got)
         to_messages(push_tiles(there), back)
@@ -462,10 +565,13 @@
         slots_wait(back, slots_in, slots_got)
         for c, part in enumerate(from_messages(back)):
             pushes[pl.ds(c * SROW, SROW), :] = part
-        contact[...] = scatter(pushes, SROW, slot_high, 0, onehot, IDXROW // 2, NROW)
+        contact[...] = scatter(
+            pushes, halved, SROW, slot_high, 0, onehot, IDXROW // 2, NROW
+        )
         update()
         for sub_no in range(1, SUBS):
             send_edges(back)
+            own_corners()
             element_stage(back, sub_no)
             return_stage(back)
             update()
@@ -506,34 +612,49 @@
 ):
     times = STEPS * SUBS
     vmem = pl.BlockSpec(memory_space=pltpu.VMEM)
-    smem = pl.BlockSpec(memory_space=pltpu.SMEM)
+    apart = pl.BlockSpec(memory_space=pltpu.HBM)
     dma = pltpu.SemaphoreType.DMA
     shape = jax.ShapeDtypeStruct(coords.shape, F32)
     rows = lambda count, kind=F32: pltpu.VMEM((count, LANES), kind)
+    field = pltpu.VMEM(coords.shape, F32)
     edges = pltpu.VMEM((times, 4, 3 * HROW, LANES), F32)
     messages = pltpu.VMEM((times, DEVS, 1, LANES), F32)
     return pl.pallas_call(
         body,
         out_shape=(shape, shape),
-        in_specs=[vmem] * 10 + [smem] * 3,
+        in_specs=[apart] * 13,
         out_specs=(vmem, vmem),
         scratch_shapes=[
+            field,
+            field,
+            field,
+            field,
+            pltpu.VMEM(elem_nodes.shape, I32),
+            pltpu.VMEM(halo_lists.shape, I32),
+            rows(NROW),
+            rows(EROW),
+            rows(CROW, I32),
+            rows(CROW, I32),
+            pltpu.VMEM(stiffness.shape, F32),
+            pltpu.SMEM(block_class.shape, I32),
+            pltpu.SMEM(tile_pairs.shape, I32),
             rows(3 * NROW),
             rows(3 * NROW),
             rows(3 * NROW),
             rows(3 * NROW),
             rows(EROW, I32),
+            rows(12 * 16),
             rows(IDXROW, I32),
             rows(IDXROW, I32),
-            rows(3 * XROW),
             rows(12 * EROW),
             rows(12 * EROW),
+            rows(12 * EROW),
+            rows(24 * EROW),
             rows(3 * NROW),
             rows(3 * NROW),
             rows(12 * HROW),
-            pltpu.VMEM(((IDXROW + SROW) // 2, 2 * LANES, LANES), BF16),
-            pltpu.VMEM((CROW, DEVS, LANES), BF16),
-            rows(CROW, I32),
+            rows(12 * HROW),
+            pltpu.VMEM(((IDXROW + SROW) // 2, 2 * LANES, 2 * LANES), BF16),
             rows(2 * DEVS),
             rows(SROW, I32),
             rows(SROW, I32),
@@ -546,6 +667,7 @@
             edges,
             messages,
             messages,
+            dma((13,)),
             dma((times, 4)),
             dma((times, 4)),
             dma((times, 4)),
@@ -554,7 +676,7 @@
             dma((times,)),
         ],
         compiler_params=pltpu.CompilerParams(
-            collective_id=0, has_side_effects=True, vmem_limit_bytes=40 * 1024 * 1024
+            collective_id=0, has_side_effects=True, vmem_limit_bytes=60 * 1024 * 1024
         ),
     )(
         coords,

time: 117 us -> 81.4 us (0.70)
  Pallas kernels: 106 us -> 78.3 us
  local copies, waits for them, and re-layouts: 9.86 us -> 2 us
    pallas_call x1, Pallas kernels: 106 us -> 78.3 us  [device_step(): pl.pallas_call(body, out_shape=(shape, shape), in_specs=[apart] * 13, out...]
    unnamed x28 -> x4, local copies, waits for them, and re-layouts: 9.86 us -> 2 us
where the time goes in v2:
time: 81.4 us; the launch traced here: 80.9 us
  Pallas kernels  78.3 us (96%)
  local copies, waits for them, and re-layouts  2 us (2%)
    pallas_call x1, Pallas kernels, device_step(): pl.pallas_call(body, out_shape=(shape, shape), in_specs=[apart] * 13, out...  78.3 us
    unnamed x4, local copies, waits for them, and re-layouts  2 us

profile of v2, /device:TPU:2, one launch (start us, length us, event | category | flops | bytes accessed | tf_op | source)
XLA Modules:
  0.0 80.9 jit_solution(10755248247199051208)
XLA Ops:
  0.6 78.3 %shard_map.140 = (f32[3,2048]{1,0:T(4,128)}, f32[3,2048]{1,0:T(4,128)}) custom-call(f32[3,2048]{1,0:T(4,128)} %coords_hbm.1, f32[3,2048]{1,0:T(4,128)} %displacement_hbm.1, f32[3,2048]{1,0:T(4,128)} %velocity_hbm.1, f32[3,2048]{1,0:T(4,128)} %ext_force_hbm.1, s32[4,2048]{1,0:T(4,128)} %elem_nodes_hbm.1, s32[4,512]{1,0:T(4,128)} %halo_lists_hbm.1, ...), custom_call_target="tpu_custom_call" | custom-call | tf_op jit(solution)/shard_map/pallas_call | solution.py:622
  78.9 0.0 copy-start
  78.9 1.4 %copy.17 = f32[3,2048]{1,0:T(4,128)} copy(f32[3,2048]{1,0:T(4,128)} %get-tuple-element.4) | data formatting | bytes 49152
  80.3 0.0 copy-done
  80.3 0.6 copy.18
Async XLA Ops:
  78.9 1.4 %copy-start = (f32[3,2048]{1,0:T(4,128)S(1)}, f32[3,2048]{1,0:T(4,128)}, u32[]{:S(2)}) copy-start(f32[3,2048]{1,0:T(4,128)} %get-tuple-element.5) | copy-start | bytes 73732

commit v3 on v2

--- a/solution.py
+++ b/solution.py
@@ -27,7 +27,8 @@
 CAP = 32
 PAIRS = 16
 IDXROW = 4 * EROW + 4 * HROW
-UNROLL = 4
+UNROLL = 16
+PAIR_UNROLL = 4
 
 F32 = jnp.float32
 BF16 = jnp.bfloat16
@@ -44,30 +45,36 @@
 
 
 def gather(tables, place, rows, high, first, onehot, number, found, target, add):
+    unroll = min(UNROLL, rows // 2)
     numbers = iota((NROW, LANES), 0) + place
 
     def some(step, carry):
-        for inner in range(UNROLL):
-            tile = step * UNROLL + inner
-            both = jnp.dot(tables, onehot[number + tile], preferred_element_type=F32)
+        for inner in range(unroll):
+            tile = step * unroll + inner
+            both = jnp.dot(
+                tables, onehot[number + tile], preferred_element_type=F32
+            )
             for side in range(2):
                 row = tile * 2 + side
                 here = jnp.broadcast_to(high[pl.ds(first + row, 1), :], (NROW, LANES)) == numbers
+                lane = slice(side * LANES, (side + 1) * LANES)
                 for c in range(3):
-                    part = both[c * NROW : (c + 1) * NROW, side * LANES : (side + 1) * LANES]
+                    upper = both[c * NROW : (c + 1) * NROW, lane]
+                    part = upper + both[(c + 3) * NROW : (c + 4) * NROW, lane]
                     total = jnp.sum(jnp.where(here, part, 0.0), axis=0, keepdims=True)
                     spot = pl.ds(target + c * rows + row, 1)
                     found[spot, :] = found[spot, :] + total if add else total
         return carry
 
-    lax.fori_loop(0, rows // (2 * UNROLL), some, 0)
+    lax.fori_loop(0, rows // (2 * unroll), some, 0)
 
 
 def split_table(table):
-    return jnp.concatenate(halves(table), axis=1).astype(BF16)
+    return jnp.concatenate(halves(table), axis=0).astype(BF16)
 
 
 def scatter(values, halved, rows, high, first, onehot, number, height):
+    unroll = min(UNROLL, rows // 2)
     upper, lower = halves(values[pl.ds(0, 3 * rows), :])
     halved[pl.ds(0, 3 * rows), :] = upper
     halved[pl.ds(3 * rows, 3 * rows), :] = lower
@@ -75,8 +82,8 @@
 
     def some(step, total):
         columns, right = [], []
-        for inner in range(2 * UNROLL):
-            row = step * 2 * UNROLL + inner
+        for inner in range(2 * unroll):
+            row = step * 2 * unroll + inner
             mine = jnp.broadcast_to(high[pl.ds(first + row, 1), :], (16, LANES))
             mine = mine.astype(F32).astype(BF16)
             here = [mine == numbers + 16 * k for k in range(height // 16)]
@@ -87,8 +94,8 @@
                 ).astype(BF16)
                 parts += [jnp.where(mask, value, jnp.zeros_like(value)) for mask in here]
             columns.append(jnp.concatenate(parts, axis=0))
-        for inner in range(UNROLL):
-            right.append(onehot[number + step * UNROLL + inner, pl.ds(0, LANES), :])
+        for inner in range(unroll):
+            right.append(onehot[number + step * unroll + inner])
         return total + lax.dot_general(
             jnp.concatenate(columns, axis=1),
             jnp.concatenate(right, axis=1),
@@ -97,30 +104,26 @@
         )
 
     total = lax.fori_loop(
-        0, rows // (2 * UNROLL), some, jnp.zeros((6 * height, LANES), F32)
+        0, rows // (2 * unroll), some, jnp.zeros((6 * height, LANES), F32)
     )
     return total[: 3 * height] + total[3 * height :]
 
 
 def build_onehots(low, first, rows, onehot, number):
+    unroll = min(UNROLL, rows // 2)
     numbers = iota((LANES, LANES), 0)
 
     def some(step, carry):
-        for inner in range(UNROLL):
-            tile = step * UNROLL + inner
+        for inner in range(unroll):
+            tile = step * unroll + inner
             for side in range(2):
                 mine = low[pl.ds(first + tile * 2 + side, 1), :]
                 here = jnp.broadcast_to(mine, (LANES, LANES)) == numbers
                 ones = jnp.where(here, 1.0, 0.0).astype(BF16)
-                for copy in range(2):
-                    onehot[
-                        number + tile,
-                        pl.ds(copy * LANES, LANES),
-                        pl.ds(side * LANES, LANES),
-                    ] = ones
+                onehot[number + tile, :, pl.ds(side * LANES, LANES)] = ones
         return carry
 
-    lax.fori_loop(0, rows // (2 * UNROLL), some, 0)
+    lax.fori_loop(0, rows // (2 * unroll), some, 0)
 
 
 def body(
@@ -242,17 +245,29 @@
 
     barrier = pltpu.get_barrier_semaphore()
 
-    def greet(k, carry):
-        other = lax.rem(me + k, DEVS)
-        pl.semaphore_signal(
-            barrier,
-            inc=1,
-            device_id=(other // N_PY, lax.rem(other, N_PY)),
-            device_id_type=MESH,
-        )
-        return carry
-
-    lax.fori_loop(1, DEVS, greet, 0)
+    flips = [
+        j + sum((1 - 2 * lax.rem(j // (1 << b), 2)) * (1 << b) for b in range(3) if mask >> b & 1)
+        for mask in range(N_PY)
+    ]
+
+    def flip(mask):
+        return sum(lax.rem(i // (1 << b) + mask // (1 << b), 2) * (1 << b) for b in range(4))
+
+    def everyone(act):
+        def some(step, carry):
+            px = flip(N_PX - 1 - step)
+            for py in flips[::-1]:
+                act(px, py)
+            return carry
+
+        lax.fori_loop(0, N_PX - 1, some, 0)
+        for py in flips[:0:-1]:
+            act(i, py)
+
+    def greet(px, py):
+        pl.semaphore_signal(barrier, inc=1, device_id=(px, py), device_id_type=MESH)
+
+    everyone(greet)
 
     def to_rows(source, target, count, rows):
         for c in range(count):
@@ -368,19 +383,17 @@
                 ).wait()
 
     def slots_start(number):
-        def send(k, carry):
-            other = lax.rem(me + k, DEVS)
+        def send(px, py):
             pltpu.make_async_remote_copy(
-                src_ref=slots_out.at[number, other],
+                src_ref=slots_out.at[number, px * N_PY + py],
                 dst_ref=slots_in.at[number, me],
                 send_sem=slots_sent.at[number],
                 recv_sem=slots_got.at[number],
-                device_id=(other // N_PY, lax.rem(other, N_PY)),
+                device_id=(px, py),
                 device_id_type=MESH,
             ).start()
-            return carry
-
-        lax.fori_loop(1, DEVS, send, 0)
+
+        everyone(send)
         slots_in[number, me] = slots_out[number, me]
 
     def slots_wait(number, buffer, sem):
@@ -437,6 +450,11 @@
         for c, part in enumerate(from_messages(number)):
             points[pl.ds(c * SROW, SROW), :] = part
         numbers = iota((SROW, LANES), 0)
+
+        def some_pairs(step, totals):
+            for inner in range(PAIR_UNROLL):
+                totals = one_pair(step * PAIR_UNROLL + inner, totals)
+            return totals
 
         def one_pair(p, totals):
             first = tile_pairs[0, p]
@@ -465,9 +483,9 @@
             )
 
         zero = jnp.zeros((SROW, LANES), F32)
-        return lax.fori_loop(0, PAIRS, one_pair, (zero, zero, zero))
-
-    def send_edges(number):
+        return lax.fori_loop(0, PAIRS // PAIR_UNROLL, some_pairs, (zero, zero, zero))
+
+    def list_edges(number):
         gather(
             split_table(disp[...]),
             0,
@@ -485,6 +503,8 @@
                 halo_out[number, n, pl.ds(c * HROW, HROW), :] = returned[
                     pl.ds((c * 4 + n) * HROW, HROW), :
                 ]
+
+    def send_edges(number):
         exchange_start(number, halo_out, halo_in, halo_sent, halo_got)
 
     def own_corners():
@@ -546,15 +566,16 @@
 
     def major(step, carry):
         there, back = 2 * step, 2 * step + 1
+        pl.when(step == 0)(prepare_halo)
+        list_edges(there)
         send_points(there)
 
         @pl.when(step == 0)
         def _():
             pl.semaphore_wait(barrier, DEVS - 1)
 
+        send_edges(there)
         slots_start(there)
-        pl.when(step == 0)(prepare_halo)
-        send_edges(there)
         pl.when(step == 0)(prepare_rest)
         own_corners()
         element_stage(there, 0)
@@ -570,6 +591,7 @@
         )
         update()
         for sub_no in range(1, SUBS):
+            list_edges(back)
             send_edges(back)
             own_corners()
             element_stage(back, sub_no)
@@ -654,7 +676,7 @@
             rows(3 * NROW),
             rows(12 * HROW),
             rows(12 * HROW),
-            pltpu.VMEM(((IDXROW + SROW) // 2, 2 * LANES, 2 * LANES), BF16),
+            pltpu.VMEM(((IDXROW + SROW) // 2, LANES, 2 * LANES), BF16),
             rows(2 * DEVS),
             rows(SROW, I32),
             rows(SROW, I32),

time: 81.4 us -> 62.6 us (0.77)
  Pallas kernels: 78.3 us -> 59.8 us
    pallas_call x1, Pallas kernels: 78.3 us -> 59.8 us  [device_step(): pl.pallas_call(body, out_shape=(shape, shape), in_specs=[apart] * 13, out...]
where the time goes in v3:
time: 62.6 us; the launch traced here: 62.4 us
  Pallas kernels  59.8 us (96%)
  local copies, waits for them, and re-layouts  2 us (3%)
  between operations  0.65 us (1%)
    pallas_call x1, Pallas kernels, device_step(): pl.pallas_call(body, out_shape=(shape, shape), in_specs=[apart] * 13, out...  59.8 us
    unnamed x4, local copies, waits for them, and re-layouts  2 us

profile of v3, /device:TPU:2, one launch (start us, length us, event | category | flops | bytes accessed | tf_op | source)
XLA Modules:
  0.0 62.4 jit_solution(16841443687947595959)
XLA Ops:
  0.6 59.8 %shard_map.140 = (f32[3,2048]{1,0:T(4,128)}, f32[3,2048]{1,0:T(4,128)}) custom-call(f32[3,2048]{1,0:T(4,128)} %coords_hbm.1, f32[3,2048]{1,0:T(4,128)} %displacement_hbm.1, f32[3,2048]{1,0:T(4,128)} %velocity_hbm.1, f32[3,2048]{1,0:T(4,128)} %ext_force_hbm.1, s32[4,2048]{1,0:T(4,128)} %elem_nodes_hbm.1, s32[4,512]{1,0:T(4,128)} %halo_lists_hbm.1, ...), custom_call_target="tpu_custom_call" | custom-call | tf_op jit(solution)/shard_map/pallas_call | solution.py:644
  60.4 0.0 copy-start
  60.4 1.4 %copy.17 = f32[3,2048]{1,0:T(4,128)} copy(f32[3,2048]{1,0:T(4,128)} %get-tuple-element.4) | data formatting | bytes 49152
  61.8 0.0 copy-done
  61.8 0.6 copy.18
Async XLA Ops:
  60.4 1.4 %copy-start = (f32[3,2048]{1,0:T(4,128)S(1)}, f32[3,2048]{1,0:T(4,128)}, u32[]{:S(2)}) copy-start(f32[3,2048]{1,0:T(4,128)} %get-tuple-element.5) | copy-start | bytes 73732

commit v4 on v3

--- a/solution.py
+++ b/solution.py
@@ -28,7 +28,7 @@
 PAIRS = 16
 IDXROW = 4 * EROW + 4 * HROW
 UNROLL = 16
-PAIR_UNROLL = 4
+PAIR_UNROLL = 8
 
 F32 = jnp.float32
 BF16 = jnp.bfloat16
@@ -73,26 +73,28 @@
     return jnp.concatenate(halves(table), axis=0).astype(BF16)
 
 
-def scatter(values, halved, rows, high, first, onehot, number, height):
-    unroll = min(UNROLL, rows // 2)
+def halve(values, halved, rows):
     upper, lower = halves(values[pl.ds(0, 3 * rows), :])
     halved[pl.ds(0, 3 * rows), :] = upper
     halved[pl.ds(3 * rows, 3 * rows), :] = lower
-    numbers = iota((16, LANES), 0).astype(F32).astype(BF16)
+
+
+def scatter(halved, rows, high, first, onehot, number, place):
+    unroll = min(UNROLL, rows // 2)
+    numbers = (iota((NROW, LANES), 0) + place).astype(F32).astype(BF16)
 
     def some(step, total):
         columns, right = [], []
         for inner in range(2 * unroll):
             row = step * 2 * unroll + inner
-            mine = jnp.broadcast_to(high[pl.ds(first + row, 1), :], (16, LANES))
-            mine = mine.astype(F32).astype(BF16)
-            here = [mine == numbers + 16 * k for k in range(height // 16)]
+            mine = jnp.broadcast_to(high[pl.ds(first + row, 1), :], (NROW, LANES))
+            here = mine.astype(F32).astype(BF16) == numbers
             parts = []
             for part in range(6):
                 value = jnp.broadcast_to(
-                    halved[pl.ds(part * rows + row, 1), :], (16, LANES)
+                    halved[pl.ds(part * rows + row, 1), :], (NROW, LANES)
                 ).astype(BF16)
-                parts += [jnp.where(mask, value, jnp.zeros_like(value)) for mask in here]
+                parts.append(jnp.where(here, value, jnp.zeros_like(value)))
             columns.append(jnp.concatenate(parts, axis=0))
         for inner in range(unroll):
             right.append(onehot[number + step * unroll + inner])
@@ -104,9 +106,9 @@
         )
 
     total = lax.fori_loop(
-        0, rows // (2 * unroll), some, jnp.zeros((6 * height, LANES), F32)
+        0, rows // (2 * unroll), some, jnp.zeros((6 * NROW, LANES), F32)
     )
-    return total[: 3 * height] + total[3 * height :]
+    return total[: 3 * NROW] + total[3 * NROW :]
 
 
 def build_onehots(low, first, rows, onehot, number):
@@ -142,6 +144,7 @@
     tile_pairs_hbm,
     disp_out,
     vel_out,
+    accel_out,
     coords,
     displacement,
     velocity,
@@ -159,6 +162,7 @@
     disp,
     vel,
     fext,
+    last,
     slow,
     spread,
     idx_low,
@@ -536,13 +540,16 @@
             else:
                 total = jnp.where(slow[...] == 1, held[place, :], total)
             forces[place, :] = total
-        summed = scatter(forces, halved, 4 * EROW, idx_high, 0, onehot, 0, XROW)
+        halve(forces, halved, 4 * EROW)
+        summed = scatter(halved, 4 * EROW, idx_high, 0, onehot, 0, NROW)
         for c in range(3):
-            internal[pl.ds(c * NROW, NROW), :] = summed[c * XROW : c * XROW + NROW]
             for n in range(4):
-                first = c * XROW + NROW + n * HROW
+                first = (c * 4 + n) * HROW
                 back_out[number, n, pl.ds(c * HROW, HROW), :] = summed[first : first + HROW]
         exchange_start(number, back_out, back_in, back_sent, back_got)
+
+    def own_sums():
+        internal[...] = scatter(halved, 4 * EROW, idx_high, 0, onehot, 0, 0)
 
     def return_stage(number):
         exchange_wait(number, back_in, back_got)
@@ -551,8 +558,9 @@
                 returned[pl.ds(c * 4 * HROW + n * HROW, HROW), :] = back_in[
                     number, n, pl.ds(c * HROW, HROW), :
                 ]
+        halve(returned, halved, 4 * HROW)
         internal[...] = internal[...] + scatter(
-            returned, halved, 4 * HROW, idx_high, 4 * EROW, onehot, 2 * EROW, NROW
+            halved, 4 * HROW, idx_high, 4 * EROW, onehot, 2 * EROW, 0
         )
 
     def update():
@@ -560,6 +568,9 @@
         for c in range(3):
             place = pl.ds(c * NROW, NROW)
             accel = mass * (fext[place, :] - internal[place, :] + contact[place, :])
+            last[pl.ds(c * NROW, NROW), :] = disp[place, :]
+            last[pl.ds((3 + c) * NROW, NROW), :] = vel[place, :]
+            last[pl.ds((6 + c) * NROW, NROW), :] = accel
             speed = vel[place, :] + DT * accel
             vel[place, :] = speed
             disp[place, :] = disp[place, :] + DT * speed
@@ -582,19 +593,20 @@
         slots_wait(there, slots_in, slots_got)
         to_messages(push_tiles(there), back)
         slots_start(back)
+        own_sums()
         return_stage(there)
         slots_wait(back, slots_in, slots_got)
         for c, part in enumerate(from_messages(back)):
             pushes[pl.ds(c * SROW, SROW), :] = part
-        contact[...] = scatter(
-            pushes, halved, SROW, slot_high, 0, onehot, IDXROW // 2, NROW
-        )
+        halve(pushes, halved, SROW)
+        contact[...] = scatter(halved, SROW, slot_high, 0, onehot, IDXROW // 2, 0)
         update()
         for sub_no in range(1, SUBS):
             list_edges(back)
             send_edges(back)
             own_corners()
             element_stage(back, sub_no)
+            own_sums()
             return_stage(back)
             update()
         return carry
@@ -603,10 +615,9 @@
 
     for c in range(3):
         for r in range(NROW):
-            row = pl.ds(c * NROW + r, 1)
             place = pl.ds(r * LANES, LANES)
-            disp_out[pl.ds(c, 1), place] = disp[row, :]
-            vel_out[pl.ds(c, 1), place] = vel[row, :]
+            for n, out in enumerate((disp_out, vel_out, accel_out)):
+                out[pl.ds(c, 1), place] = last[pl.ds((n * 3 + c) * NROW + r, 1), :]
 
     def drain(number, carry):
         exchange_wait(number, halo_out, halo_sent)
@@ -641,11 +652,11 @@
     field = pltpu.VMEM(coords.shape, F32)
     edges = pltpu.VMEM((times, 4, 3 * HROW, LANES), F32)
     messages = pltpu.VMEM((times, DEVS, 1, LANES), F32)
-    return pl.pallas_call(
+    disp, vel, accel = pl.pallas_call(
         body,
-        out_shape=(shape, shape),
+        out_shape=(shape, shape, shape),
         in_specs=[apart] * 13,
-        out_specs=(vmem, vmem),
+        out_specs=(vmem, vmem, vmem),
         scratch_shapes=[
             field,
             field,
@@ -664,6 +675,7 @@
             rows(3 * NROW),
             rows(3 * NROW),
             rows(3 * NROW),
+            rows(9 * NROW),
             rows(EROW, I32),
             rows(12 * 16),
             rows(IDXROW, I32),
@@ -715,6 +727,8 @@
         block_class,
         tile_pairs,
     )
+    vel = vel + DT * accel
+    return disp + DT * vel, vel
 
 
 def solution(mesh):

time: 62.6 us -> 61.3 us (0.979)
  local copies, waits for them, and re-layouts: 2 us -> 0 us
  other arithmetic: 0 us -> 1.43 us
  Pallas kernels: 59.8 us -> 59 us
    unnamed x4 -> x0, local copies, waits for them, and re-layouts: 2 us -> none
    add x0 -> x1, other arithmetic: none -> 1.43 us  [device_step(): return (disp + DT * vel, vel)]
    pallas_call x1, Pallas kernels: 59.8 us -> 59 us  [device_step(): pl.pallas_call(body, out_shape=(shape, shape, shape), in_specs=[apart] *...]
where the time goes in v4:
time: 61.3 us; the launch traced here: 61.1 us
  Pallas kernels  59 us (96%)
  other arithmetic  1.43 us (2%)
  between operations  0.64 us (1%)
    pallas_call x1, Pallas kernels, device_step(): pl.pallas_call(body, out_shape=(shape, shape, shape), in_specs=[apart] *...  59 us
    add x1, other arithmetic, device_step(): return (disp + DT * vel, vel)  1.43 us

profile of v4, /device:TPU:2, one launch (start us, length us, event | category | flops | bytes accessed | tf_op | source)
XLA Modules:
  0.0 61.1 jit_solution(5548475623538311366)
XLA Ops:
  0.6 59.0 %shard_map.140 = (f32[3,2048]{1,0:T(4,128)}, f32[3,2048]{1,0:T(4,128)}, f32[3,2048]{1,0:T(4,128)}) custom-call(f32[3,2048]{1,0:T(4,128)} %coords_hbm.1, f32[3,2048]{1,0:T(4,128)} %displacement_hbm.1, f32[3,2048]{1,0:T(4,128)} %velocity_hbm.1, f32[3,2048]{1,0:T(4,128)} %ext_force_hbm.1, s32[4,2048]{1,0:T(4,128)} %elem_nodes_hbm.1, s32[4,512]{1,0:T(4,128)} %halo_lists_hbm.1, ...), custom_call_target="tpu_custom_call" | custom-call | tf_op jit(solution)/shard_map/pallas_call | solution.py:655
  59.6 1.4 %multiply_add_fusion = (f32[3,2048]{1,0:T(4,128)}, f32[3,2048]{1,0:T(4,128)}) fusion(f32[3,2048]{1,0:T(4,128)} %get-tuple-element.5, f32[3,2048]{1,0:T(4,128)} %get-tuple-element.6, f32[3,2048]{1,0:T(4,128)} %get-tuple-element.7), kind=kLoop, calls=%fused_computation | loop fusion | flops 24576 | bytes 122880 | tf_op jit(solution)/shard_map/add | solution.py:731

commit v5 on v4

--- a/solution.py
+++ b/solution.py
@@ -258,13 +258,10 @@
         return sum(lax.rem(i // (1 << b) + mask // (1 << b), 2) * (1 << b) for b in range(4))
 
     def everyone(act):
-        def some(step, carry):
-            px = flip(N_PX - 1 - step)
+        for mask in range(N_PX - 1, 0, -1):
+            px = flip(mask)
             for py in flips[::-1]:
                 act(px, py)
-            return carry
-
-        lax.fori_loop(0, N_PX - 1, some, 0)
         for py in flips[:0:-1]:
             act(i, py)
 

time: 61.3 us -> 60.6 us (0.989)
  Pallas kernels: 59 us -> 58.3 us
    pallas_call x1, Pallas kernels: 59 us -> 58.3 us  [device_step(): pl.pallas_call(body, out_shape=(shape, shape, shape), in_specs=[apart] *...]
where the time goes in v5:
time: 60.6 us; the launch traced here: 60.4 us
  Pallas kernels  58.3 us (96%)
  other arithmetic  1.43 us (2%)
  between operations  0.64 us (1%)
    pallas_call x1, Pallas kernels, device_step(): pl.pallas_call(body, out_shape=(shape, shape, shape), in_specs=[apart] *...  58.3 us
    add x1, other arithmetic, device_step(): return (disp + DT * vel, vel)  1.43 us

profile of v5, /device:TPU:2, one launch (start us, length us, event | category | flops | bytes accessed | tf_op | source)
XLA Modules:
  0.0 60.4 jit_solution(9471232909349712473)
XLA Ops:
  0.6 58.3 %shard_map.140 = (f32[3,2048]{1,0:T(4,128)}, f32[3,2048]{1,0:T(4,128)}, f32[3,2048]{1,0:T(4,128)}) custom-call(f32[3,2048]{1,0:T(4,128)} %coords_hbm.1, f32[3,2048]{1,0:T(4,128)} %displacement_hbm.1, f32[3,2048]{1,0:T(4,128)} %velocity_hbm.1, f32[3,2048]{1,0:T(4,128)} %ext_force_hbm.1, s32[4,2048]{1,0:T(4,128)} %elem_nodes_hbm.1, s32[4,512]{1,0:T(4,128)} %halo_lists_hbm.1, ...), custom_call_target="tpu_custom_call" | custom-call | tf_op jit(solution)/shard_map/pallas_call | solution.py:652
  59.0 1.4 %multiply_add_fusion = (f32[3,2048]{1,0:T(4,128)}, f32[3,2048]{1,0:T(4,128)}) fusion(f32[3,2048]{1,0:T(4,128)} %get-tuple-element.5, f32[3,2048]{1,0:T(4,128)} %get-tuple-element.6, f32[3,2048]{1,0:T(4,128)} %get-tuple-element.7), kind=kLoop, calls=%fused_computation | loop fusion | flops 24576 | bytes 122880 | tf_op jit(solution)/shard_map/add | solution.py:728

commit v6 on v5

--- a/solution.py
+++ b/solution.py
@@ -230,7 +230,7 @@
         pltpu.make_async_copy(source, target, loads.at[n])
         for n, (source, target) in enumerate(zip(sources, targets))
     ]
-    for copy in copies:
+    for copy in copies[:5]:
         copy.start()
 
     i = lax.axis_index("px")
@@ -269,6 +269,8 @@
         pl.semaphore_signal(barrier, inc=1, device_id=(px, py), device_id_type=MESH)
 
     everyone(greet)
+    for copy in copies[5:]:
+        copy.start()
 
     def to_rows(source, target, count, rows):
         for c in range(count):

time: 60.6 us -> 60.6 us (level)
  no operation moved by 1% of the time
where the time goes in v6:
time: 60.6 us; the launch traced here: 60.4 us
  Pallas kernels  58.3 us (96%)
  other arithmetic  1.43 us (2%)
  between operations  0.64 us (1%)
    pallas_call x1, Pallas kernels, device_step(): pl.pallas_call(body, out_shape=(shape, shape, shape), in_specs=[apart] *...  58.3 us
    add x1, other arithmetic, device_step(): return (disp + DT * vel, vel)  1.43 us

profile of v6, /device:TPU:2, one launch (start us, length us, event | category | flops | bytes accessed | tf_op | source)
XLA Modules:
  0.0 60.4 jit_solution(13038650263853389445)
XLA Ops:
  0.6 58.3 %shard_map.140 = (f32[3,2048]{1,0:T(4,128)}, f32[3,2048]{1,0:T(4,128)}, f32[3,2048]{1,0:T(4,128)}) custom-call(f32[3,2048]{1,0:T(4,128)} %coords_hbm.1, f32[3,2048]{1,0:T(4,128)} %displacement_hbm.1, f32[3,2048]{1,0:T(4,128)} %velocity_hbm.1, f32[3,2048]{1,0:T(4,128)} %ext_force_hbm.1, s32[4,2048]{1,0:T(4,128)} %elem_nodes_hbm.1, s32[4,512]{1,0:T(4,128)} %halo_lists_hbm.1, ...), custom_call_target="tpu_custom_call" | custom-call | tf_op jit(solution)/shard_map/pallas_call | solution.py:654
  59.0 1.4 %multiply_add_fusion = (f32[3,2048]{1,0:T(4,128)}, f32[3,2048]{1,0:T(4,128)}) fusion(f32[3,2048]{1,0:T(4,128)} %get-tuple-element.5, f32[3,2048]{1,0:T(4,128)} %get-tuple-element.6, f32[3,2048]{1,0:T(4,128)} %get-tuple-element.7), kind=kLoop, calls=%fused_computation | loop fusion | flops 24576 | bytes 122880 | tf_op jit(solution)/shard_map/add | solution.py:730
